TPU v7x, 256 devices: a whole 4x4x8 slice. The times are simulated.
256 devices in a mesh: grid: 64 (over x_lo, y, z), tm: 4 (over x_hi, core).
Axes of the slice: x: 4 (x_hi: 2, x_lo: 2; x = x_hi * 2 + x_lo), y: 4, z: 8, core: 2. Of those that a mesh axis runs over, the one named last changes fastest.
Arguments:
- temps: float32 [2048, 262144], P('tm', 'grid'), may hold values from -6 to 12
- area_weight: float32 [262144], P('grid'), may hold values from 0.3 to 1
- eofs: bfloat16 [262144, 256], P('grid'), may hold values from -0.03125 to 0.03125
Outputs:
- lag_tiles: float32 [32, 256, 256], P('tm', 'grid')
All inputs are finite; a program needn't handle non-finite values.
Results may differ from a plain program's by a relative error of at most 0.0003.
Values sent between devices are 32-bit elements; how exact they have to be, the bound alone decides.
No kernel may reach another device: no remote copies, remote signals or barrier semaphores. Data moves between devices by JAX's collectives and lax.ppermute only.
A program may use at most 64 MiB of HBM per device.

v0:
```python
import jax
import jax.numpy as jnp
from jax import lax
from jax.sharding import PartitionSpec as P

LAGS = 32


def lagged_columns(own_block, total_rows, first_lag, lag_count):
    empty = jnp.zeros((total_rows, own_block.shape[1]), jnp.float32)
    pieces = [
        lax.dynamic_update_slice_in_dim(empty, own_block, first_lag + offset, 0)
        for offset in range(lag_count)
    ]
    return jnp.concatenate(pieces, axis=1)


def tile_product(own_block, extended, first_lag, lag_count):
    shifted = lagged_columns(own_block, extended.shape[0], first_lag, lag_count)
    product = jnp.einsum("sm,sh->mh", shifted, extended, precision=lax.Precision.HIGHEST)
    return product.reshape(lag_count, own_block.shape[1], extended.shape[1])


def shards(temps, area_weight, eofs):
    hours_dev = temps.shape[0]
    hour_count = hours_dev * lax.axis_size("tm")
    column_sums = lax.psum(jnp.sum(temps, axis=0), "tm")
    column_mean = column_sums / hour_count
    anomaly = ((temps - column_mean) * area_weight).astype(jnp.bfloat16)
    partial_sums = jnp.dot(anomaly, eofs, preferred_element_type=jnp.float32)
    components = lax.psum(partial_sums, "grid")
    channels = components.shape[1]
    chan_block = channels // lax.axis_size("grid")
    chan_start = lax.axis_index("grid") * chan_block
    all_rows = lax.all_gather(components, "tm", axis=0, tiled=True)
    own_block = lax.dynamic_slice_in_dim(all_rows, chan_start, chan_block, 1)
    extended = jnp.concatenate([all_rows, jnp.zeros((LAGS - 1, channels), jnp.float32)], axis=0)
    lag_count = LAGS // lax.axis_size("tm")
    first_lag = lax.axis_index("tm") * lag_count
    lag_tiles = tile_product(own_block, extended, first_lag, lag_count)
    return lag_tiles / hour_count


def solution(mesh):
    placed = (P("tm", "grid"), P("grid"), P("grid", None))
    return jax.shard_map(
        shards, mesh=mesh, in_specs=placed, out_specs=P("tm", "grid", None), check_vma=False
    )
```

profile of v0, /device:TPU:1, one launch (start us, length us, event | category | flops | bytes accessed | tf_op | source)
XLA Modules:
  0.0 680.8 jit_solution(3333425734207268882)
XLA Ops:
  6.5 0.0 copy-start
  6.5 0.0 copy-start.1
  6.5 0.0 all-reduce.3.cloned.1.call-start
  6.5 3.9 reduce_sum.9
  10.5 13.5 %psum.14 = f32[4096]{0:T(1024)S(1)} all-reduce(f32[4096]{0:T(1024)S(1)} %reduce_sum.9), channel_id=1, replica_groups=mesh['grid'=64,'tm'=4] {'tm'}, use_global_device_ids=true, to_apply=%region_1.0 | all-reduce | flops 4096 | bytes 32768 | tf_op jit(solution)/shard_map/psum | solution.py:27
  24.0 0.0 copy-done
  24.0 0.0 copy-done.1
  24.0 5.4 fusion
  29.4 0.0 all-reduce.3.cloned.1.call-update
  29.4 0.0 all-gather.2.cloned.1.call-start
  29.5 561.3 %all-reduce.3.cloned.1.call-done = f32[512,256]{1,0:T(8,128)} async-done(((f32[512,256]{1,0:T(8,128)}), f32[512,256]{1,0:T(8,128)}) %all-reduce.3.cloned.1.call-update) | async-done | bytes 524304 | tf_op jit(solution)/shard_map/psum | solution.py:31
  590.7 0.0 all-gather.2.cloned.1.call-update
  590.8 73.3 %all-gather.2.cloned.1.call-done = f32[2048,256]{1,0:T(8,128)} async-done(((f32[512,256]{1,0:T(8,128)}), f32[2048,256]{1,0:T(8,128)}) %all-gather.2.cloned.1.call-update) | async-done | bytes 2097168 | tf_op jit(solution)/shard_map/all_gather | solution.py:35
  664.0 1.6 constant_dynamic-slice_fusion
  665.6 0.3 copy.4
  666.0 0.5 dynamic_update_slice.25
  666.5 0.5 dynamic_update_slice.26
  667.1 0.5 dynamic_update_slice.27
  667.7 0.5 dynamic_update_slice.28
  668.2 0.5 dynamic_update_slice.29
  668.8 0.5 dynamic_update_slice.30
  669.4 0.5 dynamic_update_slice.31
  669.9 0.5 dynamic_update_slice.24
  670.5 0.2 concatenate.6
  670.6 2.7 fusion.5
  673.3 0.6 div.18
  (9 shorter events, 0.1 us)
Async XLA Ops:
  6.5 17.4 %copy-start = (bf16[4096,256]{1,0:T(8,128)(2,1)S(1)}, bf16[4096,256]{1,0:T(8,128)(2,1)}, u32[]{:S(2)}) copy-start(bf16[4096,256]{1,0:T(8,128)(2,1)} %param.5) | copy-start | bytes 6291460
  6.5 17.4 %copy-start.1 = (f32[4096]{0:T(1024)S(1)}, f32[4096]{0:T(1024)}, u32[]{:S(2)}) copy-start(f32[4096]{0:T(1024)} %param.4) | copy-start | bytes 49156
  6.5 584.2 %all-reduce.3.cloned.1.call-start = ((), (), s32[]{:S(2)}) async-start(), calls=%async_computation | async-start | bytes 1048576 | tf_op jit(solution)/shard_map/psum | solution.py:31
  29.4 634.6 %all-gather.2.cloned.1.call-start = ((), (), s32[]{:S(2)}) async-start(), calls=%async_computation.1 | async-start | bytes 2621440 | tf_op jit(solution)/shard_map/all_gather | solution.py:35
Sparse Core Ops, SparseCore 0:
  29.5 561.1 all-reduce.2
  592.7 71.3 all-gather.1
where the time goes:
time: 681 us
  waiting for transfers between devices  635 us (93%)
  between operations  13.6 us (2%)
  blocking collectives  13.5 us (2%)
  matrix products  8.09 us (1%)
  local copies, waits for them, and re-layouts  7.09 us (1%)
    psum x1, waiting for transfers between devices, shards(): components = lax.psum(partial_sums, 'grid')  561 us
    all_gather x1, waiting for transfers between devices, shards(): all_rows = lax.all_gather(components, 'tm', axis=0, tiled=True)  73.3 us
  transfers between devices with their start and end apart: 2, of which 2 were waited for; matrix products, arithmetic and copies ran while one was open for 0% of the time, Pallas kernels for 0%

commit v1 on v0

v1 whole, which is shorter than its diff:
```python
import jax
import jax.numpy as jnp
from jax import lax
from jax.experimental import pallas as pl
from jax.experimental.pallas import tpu as pltpu
from jax.sharding import Mesh, PartitionSpec as P

AXES = ("xl", "y", "z", "xh", "core")
SIZES = (2, 4, 8, 2, 2)
COL_BLOCK = 512
HOURS = 2048
HOURS_DEV = 512
CHANNELS = 256
LAGS_DEV = 8
TILE = 32
VMEM_SPEC = pl.BlockSpec(memory_space=pltpu.VMEM)
SMEM_SPEC = pl.BlockSpec(memory_space=pltpu.SMEM)


def project_kernel(temps_ref, weight_ref, eofs_ref, out_ref, acc_ref, mean_ref):
    step = pl.program_id(0)

    @pl.when(step == 0)
    def _():
        acc_ref[...] = jnp.zeros_like(acc_ref)
        mean_ref[...] = jnp.zeros_like(mean_ref)

    temps = temps_ref[...]
    weight = weight_ref[...]
    eofs = eofs_ref[...]
    block_mean = jnp.sum(temps, axis=0, keepdims=True) * (1.0 / HOURS_DEV)
    anomaly = (temps - block_mean) * weight
    high = anomaly.astype(jnp.bfloat16)
    low = (anomaly - high.astype(jnp.float32)).astype(jnp.bfloat16)
    acc_ref[...] += jnp.dot(high, eofs, preferred_element_type=jnp.float32) + jnp.dot(
        low, eofs, preferred_element_type=jnp.float32
    )
    level = block_mean * weight
    first = level.astype(jnp.bfloat16).astype(jnp.float32)
    second = (level - first).astype(jnp.bfloat16).astype(jnp.float32)
    third = level - first - second
    row = lax.broadcasted_iota(jnp.int32, (16, level.shape[1]), 0)
    terms = jnp.where(row == 0, first, jnp.where(row == 1, second, jnp.where(row == 2, third, 0.0)))
    mean_ref[...] += jnp.dot(terms.astype(jnp.bfloat16), eofs, preferred_element_type=jnp.float32)

    @pl.when(step == pl.num_programs(0) - 1)
    def _():
        offset = jnp.sum(mean_ref[...], axis=0, keepdims=True)
        out_ref[...] = (acc_ref[...] + offset).T


def project(temps, area_weight, eofs):
    cols = temps.shape[1]
    return pl.pallas_call(
        project_kernel,
        grid=(cols // COL_BLOCK,),
        in_specs=[
            pl.BlockSpec((HOURS_DEV, COL_BLOCK), lambda k: (0, k)),
            pl.BlockSpec((1, COL_BLOCK), lambda k: (0, k)),
            pl.BlockSpec((COL_BLOCK, CHANNELS), lambda k: (k, 0)),
        ],
        out_specs=pl.BlockSpec((CHANNELS, HOURS_DEV), lambda k: (0, 0)),
        out_shape=jax.ShapeDtypeStruct((CHANNELS, HOURS_DEV), jnp.float32),
        scratch_shapes=[
            pltpu.VMEM((HOURS_DEV, CHANNELS), jnp.float32),
            pltpu.VMEM((16, CHANNELS), jnp.float32),
        ],
        compiler_params=pltpu.CompilerParams(dimension_semantics=("arbitrary",)),
        name="project",
    )(temps, area_weight.reshape(1, cols), eofs)


def sum_rows_kernel(parts_ref, out_ref):
    total = jnp.sum(parts_ref[...], axis=0)
    for owner in range(8):
        for seg in range(4):
            out_ref[owner, seg * 4 : seg * 4 + 4, :] = total[owner * 4 : owner * 4 + 4, seg * 128 : seg * 128 + 128]


def sum_rows(parts):
    return pl.pallas_call(
        sum_rows_kernel,
        in_specs=[VMEM_SPEC],
        out_specs=VMEM_SPEC,
        out_shape=jax.ShapeDtypeStruct((8, 16, 128), jnp.float32),
        name="sum_rows",
    )(parts)


def place(block, dest_ref):
    for source in range(16):
        chan, half = source // 2, source % 2
        for core in range(2):
            for seg in range(4):
                row = core * 16 + seg * 4
                hour = ((half * 2 + core) * 4 + seg) * 128
                dest_ref[chan * 4 : chan * 4 + 4, hour : hour + 128] = block[source, row : row + 4, :]


def tiles_kernel(where_ref, mine_ref, other_ref, out_ref, a_ref, b_ref, shifted_ref):
    core = where_ref[0]
    first_lag = where_ref[1]
    mine = mine_ref[...]
    other = other_ref[...]
    place(jnp.where(core == 0, mine, other), a_ref)
    place(jnp.where(core == 0, other, mine), b_ref)
    a = a_ref[...]
    a = a - jnp.sum(a, axis=1, keepdims=True) * (1.0 / HOURS)
    b = b_ref[:, :HOURS]
    b_ref[:, :HOURS] = b - jnp.sum(b, axis=1, keepdims=True) * (1.0 / HOURS)
    b_ref[:, HOURS:] = jnp.zeros((TILE, 128), jnp.float32)
    width = HOURS + 128
    ext = pltpu.roll(b_ref[...], jnp.where(first_lag == 0, 0, width - first_lag), 1)
    for lag in range(LAGS_DEV):
        if lag:
            ext = pltpu.roll(ext, width - 1, 1)
        shifted_ref[lag * TILE : (lag + 1) * TILE, :] = ext[:, :HOURS]
    tile = lax.dot_general(
        a,
        shifted_ref[...],
        (((1,), (1,)), ((), ())),
        precision=lax.Precision.HIGHEST,
        preferred_element_type=jnp.float32,
    ) * (1.0 / HOURS)
    for owner in range(8):
        for half in range(2):
            out_ref[owner, half * 4 : half * 4 + 4, :] = tile[owner * 4 : owner * 4 + 4, half * 128 : half * 128 + 128]


def tiles(where, mine, other):
    return pl.pallas_call(
        tiles_kernel,
        in_specs=[SMEM_SPEC, VMEM_SPEC, VMEM_SPEC],
        out_specs=VMEM_SPEC,
        out_shape=jax.ShapeDtypeStruct((8, 8, 128), jnp.float32),
        scratch_shapes=[
            pltpu.VMEM((TILE, HOURS), jnp.float32),
            pltpu.VMEM((TILE, HOURS + 128), jnp.float32),
            pltpu.VMEM((LAGS_DEV * TILE, HOURS), jnp.float32),
        ],
        name="tiles",
    )(where, mine, other)


def spread_kernel(parts_ref, out_ref):
    for lag in range(LAGS_DEV):
        row, lane = 4 * (lag // 4), TILE * (lag % 4)
        for source in range(8):
            out_ref[lag, :, source * TILE : (source + 1) * TILE] = parts_ref[source, row : row + 4, lane : lane + TILE]


def spread(parts):
    return pl.pallas_call(
        spread_kernel,
        in_specs=[VMEM_SPEC],
        out_specs=VMEM_SPEC,
        out_shape=jax.ShapeDtypeStruct((LAGS_DEV, 4, CHANNELS), jnp.float32),
        name="spread",
    )(parts)


def device(i, z, xh, core):
    return ((i * 8 + z) * 2 + xh) * 2 + core


GATHER_GROUPS = [[device(i, z, xh, 0) for i in range(8) for xh in range(2)] for z in range(8)] + [
    [device(i, z, xh, 1) for z in range(8) for xh in range(2)] for i in range(8)
]
SWAP = [(0, 1), (1, 0)]


def shards(temps, area_weight, eofs):
    partial_sums = project(temps, area_weight, eofs)
    parts = lax.all_to_all(partial_sums.reshape(8, TILE, HOURS_DEV), ("xl", "y"), 0, 0)
    parts = lax.all_to_all(sum_rows(parts), "z", 0, 0)
    piece = jnp.sum(parts, axis=0)
    core = lax.axis_index("core")
    neighbour = lax.ppermute(piece, "core", SWAP)
    pair = jnp.where(
        core == 0,
        jnp.concatenate([piece, neighbour], axis=0),
        jnp.concatenate([neighbour, piece], axis=0),
    )
    mine = lax.all_to_all(
        jnp.broadcast_to(pair[None], (16, 32, 128)), AXES, 0, 0, axis_index_groups=GATHER_GROUPS
    )
    other = lax.ppermute(mine, "core", SWAP)
    first_lag = (lax.axis_index("xh") * 2 + core) * LAGS_DEV
    where = jnp.stack([core, first_lag]).astype(jnp.int32)
    out = lax.all_to_all(tiles(where, mine, other), ("xl", "y"), 0, 0)
    return spread(out)


def solution(mesh):
    fine = Mesh(mesh.devices.reshape(SIZES), AXES)
    grid, tm = ("xl", "y", "z"), ("xh", "core")
    return jax.shard_map(
        shards,
        mesh=fine,
        in_specs=(P(tm, grid), P(grid), P(grid, None)),
        out_specs=P(tm, grid, None),
        check_vma=False,
    )
```

time: 681 us -> 78.5 us (0.12)
  waiting for transfers between devices: 635 us -> 1.69 us
  blocking collectives: 13.5 us -> 54 us
  Pallas kernels: 0 us -> 16.9 us
  between operations: 13.6 us -> 0.02 us
  matrix products: 8.09 us -> 0 us
    psum x1 -> x0, waiting for transfers between devices: 561 us -> none  [shards(): components = lax.psum(partial_sums, 'grid')]
    all_gather x1 -> x0, waiting for transfers between devices: 73.3 us -> none  [shards(): all_rows = lax.all_gather(components, 'tm', axis=0, tiled=True)]
    all_to_all x0 -> x4, blocking collectives: none -> 54 us  [the longest x1 16 us: shards(): parts = lax.all_to_all(sum_rows(parts), 'z', 0, 0)]
    pallas_call x0 -> x4, Pallas kernels: none -> 16.9 us  [the longest x1 9.48 us: project(): pl.pallas_call(project_kernel, grid=(cols // COL_BLOCK,), in_specs=[pl.Bl...]
    psum x1 -> x0, blocking collectives: 13.5 us -> none  [shards(): column_sums = lax.psum(jnp.sum(temps, axis=0), 'tm')]
    dot_general x2 -> x0, matrix products: 8.09 us -> none  [the longest x1 5.43 us: shards(): partial_sums = jnp.dot(anomaly, eofs, preferred_element_type=jnp.float32)]
  transfers between devices with their start and end apart: 2 -> 2, of which waited for: 2 -> 2; matrix products, arithmetic and copies ran while one was open for 0% -> 1% of each run, Pallas kernels for 0% -> 0%
where the time goes in v1:
time: 78.5 us; the launch traced here: 77.8 us
  blocking collectives  54 us (69%)
  Pallas kernels  16.9 us (22%)
  starting transfers between devices  3.83 us (5%)
  waiting for transfers between devices  1.69 us (2%)
    all_to_all x1, blocking collectives, shards(): parts = lax.all_to_all(sum_rows(parts), 'z', 0, 0)  16 us
    all_to_all x1, blocking collectives, shards(): lax.all_to_all(jnp.broadcast_to(pair[None], (16, 32, 128)), AXES, 0, 0, a...  14.7 us
    all_to_all x1, blocking collectives, shards(): lax.all_to_all(partial_sums.reshape(8, TILE, HOURS_DEV), ('xl', 'y'), 0, 0)  14.2 us
    pallas_call x1, Pallas kernels, project(): pl.pallas_call(project_kernel, grid=(cols // COL_BLOCK,), in_specs=[pl.Bl...  9.48 us
    all_to_all x1, blocking collectives, shards(): out = lax.all_to_all(tiles(where, mine, other), ('xl', 'y'), 0, 0)  9.05 us
    pallas_call x1, Pallas kernels, tiles(): pl.pallas_call(tiles_kernel, in_specs=[SMEM_SPEC, VMEM_SPEC, VMEM_SPEC],...  4.28 us
    ppermute x1, starting transfers between devices, shards(): neighbour = lax.ppermute(piece, 'core', SWAP)  3.82 us
    pallas_call x1, Pallas kernels, sum_rows(): pl.pallas_call(sum_rows_kernel, in_specs=[VMEM_SPEC], out_specs=VMEM_SPEC...  1.69 us
  transfers between devices with their start and end apart: 2, of which 2 were waited for; matrix products, arithmetic and copies ran while one was open for 1% of the time, Pallas kernels for 0%

profile of v1, /device:TPU:1, one launch (start us, length us, event | category | flops | bytes accessed | tf_op | source)
XLA Modules:
  0.0 77.8 jit_solution(5686699724382018752)
XLA Ops:
  0.0 9.5 %project.1 = f32[256,512]{1,0:T(8,128)} custom-call(f32[512,4096]{1,0:T(8,128)} %temps_ref.1, f32[1,4096]{1,0:T(1,128)} %bitcast.5, bf16[4096,256]{1,0:T(8,128)(2,1)} %eofs_ref.1), custom_call_target="tpu_custom_call" | custom-call | tf_op jit(solution)/shard_map/project/pallas_call | solution.py:54
  9.5 14.2 %all_to_all.20.parts_ref = f32[8,32,512]{2,1,0:T(8,128)} all-to-all(f32[8,32,512]{2,1,0:T(8,128)} %bitcast.4), channel_id=1, replica_groups=mesh['xl'=2,'y'=4,'z'=8,'xh'=2,'core'=2] {'xl','y'}, dimensions={0} | all-to-all | bytes 1048576 | tf_op jit(solution)/shard_map/all_to_all | solution.py:174
  23.7 1.7 %sum_rows.1 = f32[8,16,128]{2,1,0:T(8,128)} custom-call(f32[8,32,512]{2,1,0:T(8,128)} %all_to_all.20.parts_ref), custom_call_target="tpu_custom_call" | custom-call | tf_op jit(solution)/shard_map/sum_rows/pallas_call | solution.py:81
  25.4 16.0 %all_to_all.21 = f32[8,16,128]{2,1,0:T(8,128)S(1)} all-to-all(f32[8,16,128]{2,1,0:T(8,128)} %sum_rows.1), channel_id=1, replica_groups=mesh['xl'=2,'y'=4,'z'=8,'xh'=2,'core'=2] {'z'}, dimensions={0} | all-to-all | bytes 131072 | tf_op jit(solution)/shard_map/all_to_all | solution.py:175
  41.4 3.8 %collective-permute-start = (f32[16,128]{1,0:T(8,128)S(1)}, f32[16,128]{1,0:T(8,128)S(1)}, u32[]{:S(2)}, u32[]{:S(2)}) collective-permute-start(f32[16,128]{1,0:T(8,128)S(1)} %reduce_sum.9), channel_id=1, source_target_pairs={{0,1},{1,0},{2,3},{3,2},{4,5},{5,4},{6,7},{7,6},{8,9},{9,8},{10,11... | collective-permute-start | bytes 24584 | tf_op jit(solution)/shard_map/ppermute | solution.py:178
  45.2 0.8 %collective-permute-done = f32[16,128]{1,0:T(8,128)S(1)} collective-permute-done((f32[16,128]{1,0:T(8,128)S(1)}, f32[16,128]{1,0:T(8,128)S(1)}, u32[]{:S(2)}, u32[]{:S(2)}) %collective-permute-start) | collective-permute-done | bytes 8224 | tf_op jit(solution)/shard_map/ppermute | solution.py:178
  46.1 14.7 %all_to_all.22.mine_ref = f32[16,32,128]{2,1,0:T(8,128)S(1)} all-to-all(f32[16,32,128]{2,1,0:T(8,128)S(1)} %broadcast_in_dim.2), channel_id=1, replica_groups={{0,2,32,34,64,66,96,98,128,130,160,162,192,194,224,226},{4,6,36,38,68,7..., dimensions={0} | all-to-all | bytes 524288 | tf_op jit(solution)/shard_map/all_to_all | solution.py:184
  60.8 0.0 copy-start
  60.8 0.0 collective-permute-start.1
  60.8 0.7 pad_add_fusion.where_ref
  61.5 0.9 %collective-permute-done.1.other_ref = f32[16,32,128]{2,1,0:T(8,128)S(1)} collective-permute-done((f32[16,32,128]{2,1,0:T(8,128)S(1)}, f32[16,32,128]{2,1,0:T(8,128)S(1)}, u32[]{:S(2)}, u32[]{:S(2)}) %collective-permute-start.1) | collective-permute-done | bytes 262176 | tf_op jit(solution)/shard_map/ppermute | solution.py:187
  62.3 0.0 copy-done
  62.3 0.0 copy-start.1
  62.3 0.7 copy-done.1
  63.0 4.3 %tiles.1 = f32[8,8,128]{2,1,0:T(8,128)} custom-call(s32[2]{0:T(128)} %pad_add_fusion.where_ref, f32[16,32,128]{2,1,0:T(8,128)} %copy-done, f32[16,32,128]{2,1,0:T(8,128)} %copy-done.1), custom_call_target="tpu_custom_call" | custom-call | tf_op jit(solution)/shard_map/tiles/pallas_call | solution.py:131
  67.3 9.0 %all_to_all.23.parts_ref = f32[8,8,128]{2,1,0:T(8,128)} all-to-all(f32[8,8,128]{2,1,0:T(8,128)} %tiles.1), channel_id=1, replica_groups=mesh['xl'=2,'y'=4,'z'=8,'xh'=2,'core'=2] {'xl','y'}, dimensions={0} | all-to-all | bytes 65536 | tf_op jit(solution)/shard_map/all_to_all | solution.py:190
  76.4 1.5 %spread.1 = f32[8,4,256]{2,1,0:T(4,128)} custom-call(f32[8,8,128]{2,1,0:T(8,128)} %all_to_all.23.parts_ref), custom_call_target="tpu_custom_call" | custom-call | tf_op jit(solution)/shard_map/spread/pallas_call | solution.py:153
  (3 shorter events, 0.0 us)
Async XLA Ops:
  41.4 4.7 %collective-permute-start = (f32[16,128]{1,0:T(8,128)S(1)}, f32[16,128]{1,0:T(8,128)S(1)}, u32[]{:S(2)}, u32[]{:S(2)}) collective-permute-start(f32[16,128]{1,0:T(8,128)S(1)} %reduce_sum.9), channel_id=1, source_target_pairs={{0,1},{1,0},{2,3},{3,2},{4,5},{5,4},{6,7},{7,6},{8,9},{9,8},{10,11... | collective-permute-start | bytes 24584 | tf_op jit(solution)/shard_map/ppermute | solution.py:178
  60.8 1.5 %copy-start = (f32[16,32,128]{2,1,0:T(8,128)}, f32[16,32,128]{2,1,0:T(8,128)S(1)}, u32[]{:S(2)}) copy-start(f32[16,32,128]{2,1,0:T(8,128)S(1)} %all_to_all.22.mine_ref) | copy-start | bytes 786436
  60.8 1.5 %collective-permute-start.1 = (f32[16,32,128]{2,1,0:T(8,128)S(1)}, f32[16,32,128]{2,1,0:T(8,128)S(1)}, u32[]{:S(2)}, u32[]{:S(2)}) collective-permute-start(f32[16,32,128]{2,1,0:T(8,128)S(1)} %all_to_all.22.mine_ref), channel_id=1, source_target_pairs={{0,1},{1,0},{2,3},{3,2},{4,5},{5,4},{6,7},{7,6},{8,9},{9,8},{10,11... | collective-permute-start | bytes 786440 | tf_op jit(solution)/shard_map/ppermute | solution.py:187
  62.3 0.7 copy-start.1

commit v2 on v1

v2 whole, which is shorter than its diff:
```python
import jax
import jax.numpy as jnp
from jax import lax
from jax.experimental import pallas as pl
from jax.experimental.pallas import tpu as pltpu
from jax.sharding import Mesh, PartitionSpec as P

AXES = ("xl", "y", "z", "xh", "core")
SIZES = (2, 4, 8, 2, 2)
COL_BLOCK = 512
ROW_BLOCK = 256
COPIES_AHEAD = 4
HOURS = 2048
HOURS_DEV = 512
CHANNELS = 256
LAGS_DEV = 8
TILE = 32
VMEM_SPEC = pl.BlockSpec(memory_space=pltpu.VMEM)
ANY_SPEC = pl.BlockSpec(memory_space=pl.ANY)


def on_chip(x):
    return pltpu.with_memory_space_constraint(x, pltpu.VMEM)


def project_kernel(temps_hbm, weight_hbm, eofs_hbm, out_ref, temps, weight, eofs, acc_ref, temps_sem, eofs_sem, weight_sem):
    blocks = temps.shape[0]
    weight_copy = pltpu.make_async_copy(weight_hbm, weight, weight_sem)
    weight_copy.start()
    temps_copies = [
        pltpu.make_async_copy(temps_hbm.at[:, pl.ds(k * COL_BLOCK, COL_BLOCK)], temps.at[k], temps_sem.at[k])
        for k in range(blocks)
    ]
    eofs_copies = [
        pltpu.make_async_copy(eofs_hbm.at[pl.ds(k * COL_BLOCK, COL_BLOCK), :], eofs.at[k], eofs_sem.at[k])
        for k in range(blocks)
    ]
    for k in range(COPIES_AHEAD):
        temps_copies[k].start()
        eofs_copies[k].start()
    weight_copy.wait()
    for k in range(blocks):
        temps_copies[k].wait()
        eofs_copies[k].wait()
        if k + COPIES_AHEAD < blocks:
            temps_copies[k + COPIES_AHEAD].start()
            eofs_copies[k + COPIES_AHEAD].start()
        first = k * (COL_BLOCK // 128)
        column_weight = jnp.concatenate(
            [weight[first + j : first + j + 1, :] for j in range(COL_BLOCK // 128)], axis=1
        )
        for row in range(0, HOURS_DEV, ROW_BLOCK):
            rows = slice(row, row + ROW_BLOCK)
            weighted = temps[k, rows, :] * column_weight
            high = weighted.astype(jnp.bfloat16)
            low = (weighted - high.astype(jnp.float32)).astype(jnp.bfloat16)
            product = jnp.dot(high, eofs[k], preferred_element_type=jnp.float32) + jnp.dot(
                low, eofs[k], preferred_element_type=jnp.float32
            )
            if k:
                acc_ref[rows, :] += product
            else:
                acc_ref[rows, :] = product
    out_ref[...] = acc_ref[...].T


def project(temps, area_weight, eofs):
    cols = temps.shape[1]
    blocks = cols // COL_BLOCK
    return pl.pallas_call(
        project_kernel,
        in_specs=[ANY_SPEC, ANY_SPEC, ANY_SPEC],
        out_specs=VMEM_SPEC,
        out_shape=pltpu.VMEM((CHANNELS, HOURS_DEV), jnp.float32),
        scratch_shapes=[
            pltpu.VMEM((blocks, HOURS_DEV, COL_BLOCK), jnp.float32),
            pltpu.VMEM((cols // 128, 128), jnp.float32),
            pltpu.VMEM((blocks, COL_BLOCK, CHANNELS), jnp.bfloat16),
            pltpu.VMEM((HOURS_DEV, CHANNELS), jnp.float32),
            pltpu.SemaphoreType.DMA((blocks,)),
            pltpu.SemaphoreType.DMA((blocks,)),
            pltpu.SemaphoreType.DMA(()),
        ],
        name="project",
    )(temps, area_weight.reshape(cols // 128, 128), eofs)


def sum_rows_kernel(parts_ref, out_ref):
    total = jnp.sum(parts_ref[...], axis=0)
    for owner in range(8):
        for seg in range(4):
            out_ref[owner, seg * 4 : seg * 4 + 4, :] = total[owner * 4 : owner * 4 + 4, seg * 128 : seg * 128 + 128]


def sum_rows(parts):
    return pl.pallas_call(
        sum_rows_kernel,
        in_specs=[VMEM_SPEC],
        out_specs=VMEM_SPEC,
        out_shape=pltpu.VMEM((8, 16, 128), jnp.float32),
        name="sum_rows",
    )(on_chip(parts))


def place(block, dest_ref):
    for source in range(16):
        chan, half = source // 2, source % 2
        for core in range(2):
            for seg in range(4):
                row = core * 16 + seg * 4
                hour = ((half * 2 + core) * 4 + seg) * 128
                dest_ref[chan * 4 : chan * 4 + 4, hour : hour + 128] = block[source, row : row + 4, :]


def tiles_kernel(mine_ref, other_ref, out_ref, a_ref, b_ref, shifted_ref):
    core = lax.axis_index("core")
    first_lag = (lax.axis_index("xh") * 2 + core) * LAGS_DEV
    mine = mine_ref[...]
    other = other_ref[...]
    place(jnp.where(core == 0, mine, other), a_ref)
    place(jnp.where(core == 0, other, mine), b_ref)
    a = a_ref[...]
    a = a - jnp.sum(a, axis=1, keepdims=True) * (1.0 / HOURS)
    b = b_ref[:, :HOURS]
    b_ref[:, :HOURS] = b - jnp.sum(b, axis=1, keepdims=True) * (1.0 / HOURS)
    b_ref[:, HOURS:] = jnp.zeros((TILE, 128), jnp.float32)
    width = HOURS + 128
    ext = pltpu.roll(b_ref[...], jnp.where(first_lag == 0, 0, width - first_lag), 1)
    for lag in range(LAGS_DEV):
        if lag:
            ext = pltpu.roll(ext, width - 1, 1)
        shifted_ref[lag * TILE : (lag + 1) * TILE, :] = ext[:, :HOURS]
    tile = lax.dot_general(
        a,
        shifted_ref[...],
        (((1,), (1,)), ((), ())),
        precision=lax.Precision.HIGHEST,
        preferred_element_type=jnp.float32,
    ) * (1.0 / HOURS)
    for owner in range(8):
        for half in range(2):
            out_ref[owner, half * 4 : half * 4 + 4, :] = tile[owner * 4 : owner * 4 + 4, half * 128 : half * 128 + 128]


def tiles(mine, other):
    return pl.pallas_call(
        tiles_kernel,
        in_specs=[VMEM_SPEC, VMEM_SPEC],
        out_specs=VMEM_SPEC,
        out_shape=pltpu.VMEM((8, 8, 128), jnp.float32),
        scratch_shapes=[
            pltpu.VMEM((TILE, HOURS), jnp.float32),
            pltpu.VMEM((TILE, HOURS + 128), jnp.float32),
            pltpu.VMEM((LAGS_DEV * TILE, HOURS), jnp.float32),
        ],
        name="tiles",
    )(on_chip(mine), on_chip(other))


def spread_kernel(parts_ref, out_ref):
    for lag in range(LAGS_DEV):
        row, lane = 4 * (lag // 4), TILE * (lag % 4)
        for source in range(8):
            out_ref[lag, :, source * TILE : (source + 1) * TILE] = parts_ref[source, row : row + 4, lane : lane + TILE]


def spread(parts):
    return pl.pallas_call(
        spread_kernel,
        in_specs=[VMEM_SPEC],
        out_specs=VMEM_SPEC,
        out_shape=jax.ShapeDtypeStruct((LAGS_DEV, 4, CHANNELS), jnp.float32),
        name="spread",
    )(on_chip(parts))


def device(i, z, xh, core):
    return ((i * 8 + z) * 2 + xh) * 2 + core


GATHER_GROUPS = [[device(i, z, xh, 0) for i in range(8) for xh in range(2)] for z in range(8)] + [
    [device(i, z, xh, 1) for z in range(8) for xh in range(2)] for i in range(8)
]
SWAP = [(0, 1), (1, 0)]


def shards(temps, area_weight, eofs):
    partial_sums = project(temps, area_weight, eofs)
    parts = lax.all_to_all(partial_sums.reshape(8, TILE, HOURS_DEV), ("xl", "y"), 0, 0)
    parts = lax.all_to_all(sum_rows(parts), "z", 0, 0)
    piece = jnp.sum(parts, axis=0)
    core = lax.axis_index("core")
    neighbour = lax.ppermute(piece, "core", SWAP)
    pair = jnp.where(
        core == 0,
        jnp.concatenate([piece, neighbour], axis=0),
        jnp.concatenate([neighbour, piece], axis=0),
    )
    mine = lax.all_to_all(
        jnp.broadcast_to(pair[None], (16, 32, 128)), AXES, 0, 0, axis_index_groups=GATHER_GROUPS
    )
    other = lax.ppermute(mine, "core", SWAP)
    out = lax.all_to_all(tiles(mine, other), ("xl", "y"), 0, 0)
    return spread(out)


def solution(mesh):
    fine = Mesh(mesh.devices.reshape(SIZES), AXES)
    grid, tm = ("xl", "y", "z"), ("xh", "core")
    return jax.shard_map(
        shards,
        mesh=fine,
        in_specs=(P(tm, grid), P(grid), P(grid, None)),
        out_specs=P(tm, grid, None),
        check_vma=False,
    )
```

time: 78.5 us -> 67.2 us (0.86)
  Pallas kernels: 16.9 us -> 8.76 us
  blocking collectives: 54 us -> 51.9 us
    pallas_call x2, Pallas kernels: 13.8 us -> 8 us  [the longest x1 5.37 us: project(): pl.pallas_call(project_kernel, in_specs=[ANY_SPEC, ANY_SPEC, ANY_SPEC], o...]
    pallas_call x1, Pallas kernels: 1.69 us -> 0.03 us  [sum_rows(): pl.pallas_call(sum_rows_kernel, in_specs=[VMEM_SPEC], out_specs=VMEM_SPEC...]
    all_to_all x1, blocking collectives: 9.05 us -> 7.48 us  [shards(): out = lax.all_to_all(tiles(mine, other), ('xl', 'y'), 0, 0)]
  transfers between devices with their start and end apart: 2 -> 2, of which waited for: 2 -> 2; matrix products, arithmetic and copies ran while one was open for 1% -> 0% of each run, Pallas kernels for 0% -> 0%
where the time goes in v2:
time: 67.2 us; the launch traced here: 66.9 us
  blocking collectives  51.9 us (77%)
  Pallas kernels  8.76 us (13%)
  starting transfers between devices  3.83 us (6%)
  waiting for transfers between devices  2.36 us (4%)
    all_to_all x1, blocking collectives, shards(): parts = lax.all_to_all(sum_rows(parts), 'z', 0, 0)  15.3 us
    all_to_all x1, blocking collectives, shards(): lax.all_to_all(jnp.broadcast_to(pair[None], (16, 32, 128)), AXES, 0, 0, a...  14.8 us
    all_to_all x1, blocking collectives, shards(): lax.all_to_all(partial_sums.reshape(8, TILE, HOURS_DEV), ('xl', 'y'), 0, 0)  14.4 us
    all_to_all x1, blocking collectives, shards(): out = lax.all_to_all(tiles(mine, other), ('xl', 'y'), 0, 0)  7.48 us
    pallas_call x1, Pallas kernels, project(): pl.pallas_call(project_kernel, in_specs=[ANY_SPEC, ANY_SPEC, ANY_SPEC], o...  5.37 us
    ppermute x1, starting transfers between devices, shards(): neighbour = lax.ppermute(piece, 'core', SWAP)  3.82 us
    pallas_call x1, Pallas kernels, tiles(): pl.pallas_call(tiles_kernel, in_specs=[VMEM_SPEC, VMEM_SPEC], out_specs=V...  2.63 us
    ppermute x1, waiting for transfers between devices, shards(): other = lax.ppermute(mine, 'core', SWAP)  1.53 us
  transfers between devices with their start and end apart: 2, of which 2 were waited for; matrix products, arithmetic and copies ran while one was open for 0% of the time, Pallas kernels for 0%

profile of v2, /device:TPU:1, one launch (start us, length us, event | category | flops | bytes accessed | tf_op | source)
XLA Modules:
  0.0 66.9 jit_solution(16898194583883984313)
XLA Ops:
  0.0 5.4 %project.1 = f32[256,512]{1,0:T(8,128)S(1)} custom-call(f32[512,4096]{1,0:T(8,128)} %temps_hbm.1, f32[32,128]{1,0:T(8,128)} %bitcast.3, bf16[4096,256]{1,0:T(8,128)(2,1)} %eofs_hbm.1), custom_call_target="tpu_custom_call" | custom-call | tf_op jit(solution)/shard_map/project/pallas_call | solution.py:70
  5.4 14.4 %all_to_all.20.parts_ref = f32[8,32,512]{2,1,0:T(8,128)S(1)} all-to-all(f32[8,32,512]{2,1,0:T(8,128)S(1)} %bitcast.2), channel_id=1, replica_groups=mesh['xl'=2,'y'=4,'z'=8,'xh'=2,'core'=2] {'xl','y'}, dimensions={0} | all-to-all | bytes 1048576 | tf_op jit(solution)/shard_map/all_to_all | solution.py:189
  19.8 15.3 %all_to_all.21 = f32[8,16,128]{2,1,0:T(8,128)S(1)} all-to-all(f32[8,16,128]{2,1,0:T(8,128)S(1)} %sum_rows.1), channel_id=1, replica_groups=mesh['xl'=2,'y'=4,'z'=8,'xh'=2,'core'=2] {'z'}, dimensions={0} | all-to-all | bytes 131072 | tf_op jit(solution)/shard_map/all_to_all | solution.py:190
  35.1 3.8 %collective-permute-start = (f32[16,128]{1,0:T(8,128)S(1)}, f32[16,128]{1,0:T(8,128)S(1)}, u32[]{:S(2)}, u32[]{:S(2)}) collective-permute-start(f32[16,128]{1,0:T(8,128)S(1)} %reduce_sum.9), channel_id=1, source_target_pairs={{0,1},{1,0},{2,3},{3,2},{4,5},{5,4},{6,7},{7,6},{8,9},{9,8},{10,11... | collective-permute-start | bytes 24584 | tf_op jit(solution)/shard_map/ppermute | solution.py:193
  38.9 0.8 %collective-permute-done = f32[16,128]{1,0:T(8,128)S(1)} collective-permute-done((f32[16,128]{1,0:T(8,128)S(1)}, f32[16,128]{1,0:T(8,128)S(1)}, u32[]{:S(2)}, u32[]{:S(2)}) %collective-permute-start) | collective-permute-done | bytes 8224 | tf_op jit(solution)/shard_map/ppermute | solution.py:193
  39.8 14.8 %all_to_all.22.mine_ref = f32[16,32,128]{2,1,0:T(8,128)S(1)} all-to-all(f32[16,32,128]{2,1,0:T(8,128)S(1)} %broadcast_in_dim.2), channel_id=1, replica_groups={{0,2,32,34,64,66,96,98,128,130,160,162,192,194,224,226},{4,6,36,38,68,7..., dimensions={0} | all-to-all | bytes 524288 | tf_op jit(solution)/shard_map/all_to_all | solution.py:199
  54.5 0.0 collective-permute-start.1
  54.5 1.5 %collective-permute-done.1.other_ref = f32[16,32,128]{2,1,0:T(8,128)S(1)} collective-permute-done((f32[16,32,128]{2,1,0:T(8,128)S(1)}, f32[16,32,128]{2,1,0:T(8,128)S(1)}, u32[]{:S(2)}, u32[]{:S(2)}) %collective-permute-start.1) | collective-permute-done | bytes 262176 | tf_op jit(solution)/shard_map/ppermute | solution.py:202
  56.1 2.6 %tiles.1 = f32[8,8,128]{2,1,0:T(8,128)S(1)} custom-call(f32[16,32,128]{2,1,0:T(8,128)S(1)} %all_to_all.22.mine_ref, f32[16,32,128]{2,1,0:T(8,128)S(1)} %collective-permute-done.1.other_ref), custom_call_target="tpu_custom_call" | custom-call | tf_op jit(solution)/shard_map/tiles/pallas_call | solution.py:146
  58.7 7.5 %all_to_all.23.parts_ref = f32[8,8,128]{2,1,0:T(8,128)S(1)} all-to-all(f32[8,8,128]{2,1,0:T(8,128)S(1)} %tiles.1), channel_id=1, replica_groups=mesh['xl'=2,'y'=4,'z'=8,'xh'=2,'core'=2] {'xl','y'}, dimensions={0} | all-to-all | bytes 65536 | tf_op jit(solution)/shard_map/all_to_all | solution.py:203
  66.2 0.7 %spread.1 = f32[8,4,256]{2,1,0:T(4,128)} custom-call(f32[8,8,128]{2,1,0:T(8,128)S(1)} %all_to_all.23.parts_ref), custom_call_target="tpu_custom_call" | custom-call | tf_op jit(solution)/shard_map/spread/pallas_call | solution.py:168
  (4 shorter events, 0.1 us)
Async XLA Ops:
  35.1 4.7 %collective-permute-start = (f32[16,128]{1,0:T(8,128)S(1)}, f32[16,128]{1,0:T(8,128)S(1)}, u32[]{:S(2)}, u32[]{:S(2)}) collective-permute-start(f32[16,128]{1,0:T(8,128)S(1)} %reduce_sum.9), channel_id=1, source_target_pairs={{0,1},{1,0},{2,3},{3,2},{4,5},{5,4},{6,7},{7,6},{8,9},{9,8},{10,11... | collective-permute-start | bytes 24584 | tf_op jit(solution)/shard_map/ppermute | solution.py:193
  54.5 1.5 %collective-permute-start.1 = (f32[16,32,128]{2,1,0:T(8,128)S(1)}, f32[16,32,128]{2,1,0:T(8,128)S(1)}, u32[]{:S(2)}, u32[]{:S(2)}) collective-permute-start(f32[16,32,128]{2,1,0:T(8,128)S(1)} %all_to_all.22.mine_ref), channel_id=1, source_target_pairs={{0,1},{1,0},{2,3},{3,2},{4,5},{5,4},{6,7},{7,6},{8,9},{9,8},{10,11... | collective-permute-start | bytes 786440 | tf_op jit(solution)/shard_map/ppermute | solution.py:202

commit v3 on v2

--- a/solution.py
+++ b/solution.py
@@ -112,6 +112,11 @@
                 dest_ref[chan * 4 : chan * 4 + 4, hour : hour + 128] = block[source, row : row + 4, :]
 
 
+def split(x):
+    high = x.astype(jnp.bfloat16)
+    return high, (x - high.astype(jnp.float32)).astype(jnp.bfloat16)
+
+
 def tiles_kernel(mine_ref, other_ref, out_ref, a_ref, b_ref, shifted_ref):
     core = lax.axis_index("core")
     first_lag = (lax.axis_index("xh") * 2 + core) * LAGS_DEV
@@ -126,20 +131,22 @@
     b_ref[:, HOURS:] = jnp.zeros((TILE, 128), jnp.float32)
     width = HOURS + 128
     ext = pltpu.roll(b_ref[...], jnp.where(first_lag == 0, 0, width - first_lag), 1)
-    for lag in range(LAGS_DEV):
-        if lag:
-            ext = pltpu.roll(ext, width - 1, 1)
-        shifted_ref[lag * TILE : (lag + 1) * TILE, :] = ext[:, :HOURS]
-    tile = lax.dot_general(
-        a,
-        shifted_ref[...],
-        (((1,), (1,)), ((), ())),
-        precision=lax.Precision.HIGHEST,
-        preferred_element_type=jnp.float32,
-    ) * (1.0 / HOURS)
-    for owner in range(8):
-        for half in range(2):
-            out_ref[owner, half * 4 : half * 4 + 4, :] = tile[owner * 4 : owner * 4 + 4, half * 128 : half * 128 + 128]
+    half = LAGS_DEV // 2
+    late = jnp.where(lax.broadcasted_iota(jnp.int32, a.shape, 1) < half, 0.0, pltpu.roll(a, half, 1))
+    left = jnp.concatenate([*split(a), *split(late)], axis=0)
+    for lag in range(half):
+        moved = (pltpu.roll(ext, width - lag, 1) if lag else ext)[:, :HOURS]
+        high, low = split(moved)
+        shifted_ref[lag * TILE : (lag + 1) * TILE, :] = high
+        shifted_ref[128 + lag * TILE : 128 + (lag + 1) * TILE, :] = low
+    product = lax.dot_general(
+        left, shifted_ref[...], (((1,), (1,)), ((), ())), preferred_element_type=jnp.float32
+    )
+    for p in range(2):
+        high, low = product[2 * p * TILE : (2 * p + 1) * TILE, :], product[(2 * p + 1) * TILE : (2 * p + 2) * TILE, :]
+        tile = (high[:, :128] + low[:, :128] + high[:, 128:]) * (1.0 / HOURS)
+        for owner in range(8):
+            out_ref[owner, p * 4 : p * 4 + 4, :] = tile[owner * 4 : owner * 4 + 4, :]
 
 
 def tiles(mine, other):
@@ -151,7 +158,7 @@
         scratch_shapes=[
             pltpu.VMEM((TILE, HOURS), jnp.float32),
             pltpu.VMEM((TILE, HOURS + 128), jnp.float32),
-            pltpu.VMEM((LAGS_DEV * TILE, HOURS), jnp.float32),
+            pltpu.VMEM((LAGS_DEV * TILE, HOURS), jnp.bfloat16),
         ],
         name="tiles",
     )(on_chip(mine), on_chip(other))

time: 67.2 us -> 65.4 us (0.973)
  Pallas kernels: 8.76 us -> 7.03 us
    pallas_call x1, Pallas kernels: 2.63 us -> 0.9 us  [tiles(): pl.pallas_call(tiles_kernel, in_specs=[VMEM_SPEC, VMEM_SPEC], out_specs=V...]
where the time goes in v3:
time: 65.4 us; the launch traced here: 65.2 us
  blocking collectives  51.9 us (79%)
  Pallas kernels  7.03 us (11%)
  starting transfers between devices  3.83 us (6%)
  waiting for transfers between devices  2.36 us (4%)
    all_to_all x1, blocking collectives, shards(): parts = lax.all_to_all(sum_rows(parts), 'z', 0, 0)  15.3 us
    all_to_all x1, blocking collectives, shards(): lax.all_to_all(jnp.broadcast_to(pair[None], (16, 32, 128)), AXES, 0, 0, a...  14.8 us
    all_to_all x1, blocking collectives, shards(): lax.all_to_all(partial_sums.reshape(8, TILE, HOURS_DEV), ('xl', 'y'), 0, 0)  14.4 us
    all_to_all x1, blocking collectives, shards(): out = lax.all_to_all(tiles(mine, other), ('xl', 'y'), 0, 0)  7.48 us
    pallas_call x1, Pallas kernels, project(): pl.pallas_call(project_kernel, in_specs=[ANY_SPEC, ANY_SPEC, ANY_SPEC], o...  5.37 us
    ppermute x1, starting transfers between devices, shards(): neighbour = lax.ppermute(piece, 'core', SWAP)  3.82 us
    ppermute x1, waiting for transfers between devices, shards(): other = lax.ppermute(mine, 'core', SWAP)  1.53 us
  transfers between devices with their start and end apart: 2, of which 2 were waited for; matrix products, arithmetic and copies ran while one was open for 0% of the time, Pallas kernels for 0%

profile of v3, /device:TPU:1, one launch (start us, length us, event | category | flops | bytes accessed | tf_op | source)
XLA Modules:
  0.0 65.2 jit_solution(1123577769264816025)
XLA Ops:
  0.0 5.4 %project.1 = f32[256,512]{1,0:T(8,128)S(1)} custom-call(f32[512,4096]{1,0:T(8,128)} %temps_hbm.1, f32[32,128]{1,0:T(8,128)} %bitcast.3, bf16[4096,256]{1,0:T(8,128)(2,1)} %eofs_hbm.1), custom_call_target="tpu_custom_call" | custom-call | tf_op jit(solution)/shard_map/project/pallas_call | solution.py:70
  5.4 14.4 %all_to_all.20.parts_ref = f32[8,32,512]{2,1,0:T(8,128)S(1)} all-to-all(f32[8,32,512]{2,1,0:T(8,128)S(1)} %bitcast.2), channel_id=1, replica_groups=mesh['xl'=2,'y'=4,'z'=8,'xh'=2,'core'=2] {'xl','y'}, dimensions={0} | all-to-all | bytes 1048576 | tf_op jit(solution)/shard_map/all_to_all | solution.py:196
  19.8 15.3 %all_to_all.21 = f32[8,16,128]{2,1,0:T(8,128)S(1)} all-to-all(f32[8,16,128]{2,1,0:T(8,128)S(1)} %sum_rows.1), channel_id=1, replica_groups=mesh['xl'=2,'y'=4,'z'=8,'xh'=2,'core'=2] {'z'}, dimensions={0} | all-to-all | bytes 131072 | tf_op jit(solution)/shard_map/all_to_all | solution.py:197
  35.1 3.8 %collective-permute-start = (f32[16,128]{1,0:T(8,128)S(1)}, f32[16,128]{1,0:T(8,128)S(1)}, u32[]{:S(2)}, u32[]{:S(2)}) collective-permute-start(f32[16,128]{1,0:T(8,128)S(1)} %reduce_sum.9), channel_id=1, source_target_pairs={{0,1},{1,0},{2,3},{3,2},{4,5},{5,4},{6,7},{7,6},{8,9},{9,8},{10,11... | collective-permute-start | bytes 24584 | tf_op jit(solution)/shard_map/ppermute | solution.py:200
  38.9 0.8 %collective-permute-done = f32[16,128]{1,0:T(8,128)S(1)} collective-permute-done((f32[16,128]{1,0:T(8,128)S(1)}, f32[16,128]{1,0:T(8,128)S(1)}, u32[]{:S(2)}, u32[]{:S(2)}) %collective-permute-start) | collective-permute-done | bytes 8224 | tf_op jit(solution)/shard_map/ppermute | solution.py:200
  39.8 14.8 %all_to_all.22.mine_ref = f32[16,32,128]{2,1,0:T(8,128)S(1)} all-to-all(f32[16,32,128]{2,1,0:T(8,128)S(1)} %broadcast_in_dim.2), channel_id=1, replica_groups={{0,2,32,34,64,66,96,98,128,130,160,162,192,194,224,226},{4,6,36,38,68,7..., dimensions={0} | all-to-all | bytes 524288 | tf_op jit(solution)/shard_map/all_to_all | solution.py:206
  54.5 0.0 collective-permute-start.1
  54.5 1.5 %collective-permute-done.1.other_ref = f32[16,32,128]{2,1,0:T(8,128)S(1)} collective-permute-done((f32[16,32,128]{2,1,0:T(8,128)S(1)}, f32[16,32,128]{2,1,0:T(8,128)S(1)}, u32[]{:S(2)}, u32[]{:S(2)}) %collective-permute-start.1) | collective-permute-done | bytes 262176 | tf_op jit(solution)/shard_map/ppermute | solution.py:209
  56.1 0.9 %tiles.1 = f32[8,8,128]{2,1,0:T(8,128)S(1)} custom-call(f32[16,32,128]{2,1,0:T(8,128)S(1)} %all_to_all.22.mine_ref, f32[16,32,128]{2,1,0:T(8,128)S(1)} %collective-permute-done.1.other_ref), custom_call_target="tpu_custom_call" | custom-call | tf_op jit(solution)/shard_map/tiles/pallas_call | solution.py:153
  57.0 7.5 %all_to_all.23.parts_ref = f32[8,8,128]{2,1,0:T(8,128)S(1)} all-to-all(f32[8,8,128]{2,1,0:T(8,128)S(1)} %tiles.1), channel_id=1, replica_groups=mesh['xl'=2,'y'=4,'z'=8,'xh'=2,'core'=2] {'xl','y'}, dimensions={0} | all-to-all | bytes 65536 | tf_op jit(solution)/shard_map/all_to_all | solution.py:210
  64.5 0.7 %spread.1 = f32[8,4,256]{2,1,0:T(4,128)} custom-call(f32[8,8,128]{2,1,0:T(8,128)S(1)} %all_to_all.23.parts_ref), custom_call_target="tpu_custom_call" | custom-call | tf_op jit(solution)/shard_map/spread/pallas_call | solution.py:175
  (4 shorter events, 0.1 us)
Async XLA Ops:
  35.1 4.7 %collective-permute-start = (f32[16,128]{1,0:T(8,128)S(1)}, f32[16,128]{1,0:T(8,128)S(1)}, u32[]{:S(2)}, u32[]{:S(2)}) collective-permute-start(f32[16,128]{1,0:T(8,128)S(1)} %reduce_sum.9), channel_id=1, source_target_pairs={{0,1},{1,0},{2,3},{3,2},{4,5},{5,4},{6,7},{7,6},{8,9},{9,8},{10,11... | collective-permute-start | bytes 24584 | tf_op jit(solution)/shard_map/ppermute | solution.py:200
  54.5 1.5 %collective-permute-start.1 = (f32[16,32,128]{2,1,0:T(8,128)S(1)}, f32[16,32,128]{2,1,0:T(8,128)S(1)}, u32[]{:S(2)}, u32[]{:S(2)}) collective-permute-start(f32[16,32,128]{2,1,0:T(8,128)S(1)} %all_to_all.22.mine_ref), channel_id=1, source_target_pairs={{0,1},{1,0},{2,3},{3,2},{4,5},{5,4},{6,7},{7,6},{8,9},{9,8},{10,11... | collective-permute-start | bytes 786440 | tf_op jit(solution)/shard_map/ppermute | solution.py:209

commit v4 on v3

--- a/solution.py
+++ b/solution.py
@@ -61,7 +61,19 @@
                 acc_ref[rows, :] += product
             else:
                 acc_ref[rows, :] = product
-    out_ref[...] = acc_ref[...].T
+    rows = acc_ref[...].T
+    core = lax.axis_index("core")
+
+    @pl.when(core == 0)
+    def _():
+        out_ref[...] = rows
+
+    @pl.when(core == 1)
+    def _():
+        for i in range(8):
+            for z in range(8):
+                source, dest = (i * 8 + z) * 4, (z * 8 + i) * 4
+                out_ref[dest : dest + 4, :] = rows[source : source + 4, :]
 
 
 def project(temps, area_weight, eofs):
@@ -185,6 +197,10 @@
     return ((i * 8 + z) * 2 + xh) * 2 + core
 
 
+PLANES = [[[device(i, z, xh, core) for i in range(8)] for z in range(8) for xh in range(2)] for core in range(2)]
+LINES = [[[device(i, z, xh, core) for z in range(8)] for i in range(8) for xh in range(2)] for core in range(2)]
+FIRST_GROUPS = PLANES[0] + LINES[1]
+SECOND_GROUPS = LINES[0] + PLANES[1]
 GATHER_GROUPS = [[device(i, z, xh, 0) for i in range(8) for xh in range(2)] for z in range(8)] + [
     [device(i, z, xh, 1) for z in range(8) for xh in range(2)] for i in range(8)
 ]
@@ -193,8 +209,10 @@
 
 def shards(temps, area_weight, eofs):
     partial_sums = project(temps, area_weight, eofs)
-    parts = lax.all_to_all(partial_sums.reshape(8, TILE, HOURS_DEV), ("xl", "y"), 0, 0)
-    parts = lax.all_to_all(sum_rows(parts), "z", 0, 0)
+    parts = lax.all_to_all(
+        partial_sums.reshape(8, TILE, HOURS_DEV), AXES, 0, 0, axis_index_groups=FIRST_GROUPS
+    )
+    parts = lax.all_to_all(sum_rows(parts), AXES, 0, 0, axis_index_groups=SECOND_GROUPS)
     piece = jnp.sum(parts, axis=0)
     core = lax.axis_index("core")
     neighbour = lax.ppermute(piece, "core", SWAP)

time: 65.4 us -> 64 us (0.979)
  starting transfers between devices: 3.83 us -> 0.64 us
  blocking collectives: 51.9 us -> 53.6 us
    ppermute x1, starting transfers between devices: 3.82 us -> 0.64 us  [shards(): neighbour = lax.ppermute(piece, 'core', SWAP)]
    all_to_all x2, blocking collectives: 29.7 us -> 31.4 us  [the longest x1 21 us: shards(): lax.all_to_all(partial_sums.reshape(8, TILE, HOURS_DEV), AXES, 0, 0, axis...]
where the time goes in v4:
time: 64 us; the launch traced here: 63.8 us
  blocking collectives  53.6 us (84%)
  Pallas kernels  7.11 us (11%)
  waiting for transfers between devices  2.36 us (4%)
  starting transfers between devices  0.64 us (1%)
    all_to_all x1, blocking collectives, shards(): lax.all_to_all(partial_sums.reshape(8, TILE, HOURS_DEV), AXES, 0, 0, axis...  21 us
    all_to_all x1, blocking collectives, shards(): lax.all_to_all(jnp.broadcast_to(pair[None], (16, 32, 128)), AXES, 0, 0, a...  14.7 us
    all_to_all x1, blocking collectives, shards(): lax.all_to_all(sum_rows(parts), AXES, 0, 0, axis_index_groups=SECOND_GROUPS)  10.4 us
    all_to_all x1, blocking collectives, shards(): out = lax.all_to_all(tiles(mine, other), ('xl', 'y'), 0, 0)  7.48 us
    pallas_call x1, Pallas kernels, project(): pl.pallas_call(project_kernel, in_specs=[ANY_SPEC, ANY_SPEC, ANY_SPEC], o...  5.44 us
    ppermute x1, waiting for transfers between devices, shards(): other = lax.ppermute(mine, 'core', SWAP)  1.53 us
  transfers between devices with their start and end apart: 2, of which 2 were waited for; matrix products, arithmetic and copies ran while one was open for 0% of the time, Pallas kernels for 0%

profile of v4, /device:TPU:1, one launch (start us, length us, event | category | flops | bytes accessed | tf_op | source)
XLA Modules:
  0.0 63.8 jit_solution(18006912836669261757)
XLA Ops:
  0.0 5.4 %project.1 = f32[256,512]{1,0:T(8,128)S(1)} custom-call(f32[512,4096]{1,0:T(8,128)} %temps_hbm.1, f32[32,128]{1,0:T(8,128)} %bitcast.3, bf16[4096,256]{1,0:T(8,128)(2,1)} %eofs_hbm.1), custom_call_target="tpu_custom_call" | custom-call | tf_op jit(solution)/shard_map/project/pallas_call | solution.py:82
  5.5 21.0 %all_to_all.20.parts_ref = f32[8,32,512]{2,1,0:T(8,128)S(1)} all-to-all(f32[8,32,512]{2,1,0:T(8,128)S(1)} %bitcast.2), channel_id=1, replica_groups={{0,32,64,96,128,160,192,224},{2,34,66,98,130,162,194,226},{4,36,68,100,..., dimensions={0} | all-to-all | bytes 1048576 | tf_op jit(solution)/shard_map/all_to_all | solution.py:212
  26.4 10.4 %all_to_all.21 = f32[8,16,128]{2,1,0:T(8,128)S(1)} all-to-all(f32[8,16,128]{2,1,0:T(8,128)S(1)} %sum_rows.1), channel_id=1, replica_groups={{0,4,8,12,16,20,24,28},{2,6,10,14,18,22,26,30},{32,36,40,44,48,52,56,60..., dimensions={0} | all-to-all | bytes 131072 | tf_op jit(solution)/shard_map/all_to_all | solution.py:215
  36.9 0.6 %collective-permute-start = (f32[16,128]{1,0:T(8,128)S(1)}, f32[16,128]{1,0:T(8,128)S(1)}, u32[]{:S(2)}, u32[]{:S(2)}) collective-permute-start(f32[16,128]{1,0:T(8,128)S(1)} %reduce_sum.9), channel_id=1, source_target_pairs={{0,1},{1,0},{2,3},{3,2},{4,5},{5,4},{6,7},{7,6},{8,9},{9,8},{10,11... | collective-permute-start | bytes 24584 | tf_op jit(solution)/shard_map/ppermute | solution.py:218
  37.5 0.8 %collective-permute-done = f32[16,128]{1,0:T(8,128)S(1)} collective-permute-done((f32[16,128]{1,0:T(8,128)S(1)}, f32[16,128]{1,0:T(8,128)S(1)}, u32[]{:S(2)}, u32[]{:S(2)}) %collective-permute-start) | collective-permute-done | bytes 8224 | tf_op jit(solution)/shard_map/ppermute | solution.py:218
  38.4 14.7 %all_to_all.22.mine_ref = f32[16,32,128]{2,1,0:T(8,128)S(1)} all-to-all(f32[16,32,128]{2,1,0:T(8,128)S(1)} %broadcast_in_dim.2), channel_id=1, replica_groups={{0,2,32,34,64,66,96,98,128,130,160,162,192,194,224,226},{4,6,36,38,68,7..., dimensions={0} | all-to-all | bytes 524288 | tf_op jit(solution)/shard_map/all_to_all | solution.py:224
  53.1 0.0 collective-permute-start.1
  53.1 1.5 %collective-permute-done.1.other_ref = f32[16,32,128]{2,1,0:T(8,128)S(1)} collective-permute-done((f32[16,32,128]{2,1,0:T(8,128)S(1)}, f32[16,32,128]{2,1,0:T(8,128)S(1)}, u32[]{:S(2)}, u32[]{:S(2)}) %collective-permute-start.1) | collective-permute-done | bytes 262176 | tf_op jit(solution)/shard_map/ppermute | solution.py:227
  54.6 0.9 %tiles.1 = f32[8,8,128]{2,1,0:T(8,128)S(1)} custom-call(f32[16,32,128]{2,1,0:T(8,128)S(1)} %all_to_all.22.mine_ref, f32[16,32,128]{2,1,0:T(8,128)S(1)} %collective-permute-done.1.other_ref), custom_call_target="tpu_custom_call" | custom-call | tf_op jit(solution)/shard_map/tiles/pallas_call | solution.py:165
  55.5 7.5 %all_to_all.23.parts_ref = f32[8,8,128]{2,1,0:T(8,128)S(1)} all-to-all(f32[8,8,128]{2,1,0:T(8,128)S(1)} %tiles.1), channel_id=1, replica_groups=mesh['xl'=2,'y'=4,'z'=8,'xh'=2,'core'=2] {'xl','y'}, dimensions={0} | all-to-all | bytes 65536 | tf_op jit(solution)/shard_map/all_to_all | solution.py:228
  63.0 0.7 %spread.1 = f32[8,4,256]{2,1,0:T(4,128)} custom-call(f32[8,8,128]{2,1,0:T(8,128)S(1)} %all_to_all.23.parts_ref), custom_call_target="tpu_custom_call" | custom-call | tf_op jit(solution)/shard_map/spread/pallas_call | solution.py:187
  (4 shorter events, 0.1 us)
Async XLA Ops:
  36.9 1.5 %collective-permute-start = (f32[16,128]{1,0:T(8,128)S(1)}, f32[16,128]{1,0:T(8,128)S(1)}, u32[]{:S(2)}, u32[]{:S(2)}) collective-permute-start(f32[16,128]{1,0:T(8,128)S(1)} %reduce_sum.9), channel_id=1, source_target_pairs={{0,1},{1,0},{2,3},{3,2},{4,5},{5,4},{6,7},{7,6},{8,9},{9,8},{10,11... | collective-permute-start | bytes 24584 | tf_op jit(solution)/shard_map/ppermute | solution.py:218
  53.1 1.5 %collective-permute-start.1 = (f32[16,32,128]{2,1,0:T(8,128)S(1)}, f32[16,32,128]{2,1,0:T(8,128)S(1)}, u32[]{:S(2)}, u32[]{:S(2)}) collective-permute-start(f32[16,32,128]{2,1,0:T(8,128)S(1)} %all_to_all.22.mine_ref), channel_id=1, source_target_pairs={{0,1},{1,0},{2,3},{3,2},{4,5},{5,4},{6,7},{7,6},{8,9},{9,8},{10,11... | collective-permute-start | bytes 786440 | tf_op jit(solution)/shard_map/ppermute | solution.py:227

commit v5 on v4

--- a/solution.py
+++ b/solution.py
@@ -15,6 +15,10 @@
 CHANNELS = 256
 LAGS_DEV = 8
 TILE = 32
+LINE_ORDER = (4, 3, 2, 1, 0, 7, 6, 5)
+PLANE_ORDER = (6, 5, 4, 7, 2, 1, 0, 3)
+OUT_ORDER = (6, 5, 4, 7, 2, 1, 0, 3)
+HALF_ORDER = (1, 0)
 VMEM_SPEC = pl.BlockSpec(memory_space=pltpu.VMEM)
 ANY_SPEC = pl.BlockSpec(memory_space=pl.ANY)
 
@@ -66,14 +70,15 @@
 
     @pl.when(core == 0)
     def _():
-        out_ref[...] = rows
+        for k, i in enumerate(PLANE_ORDER):
+            for m, z in enumerate(LINE_ORDER):
+                out_ref[k * 32 + m * 4 : k * 32 + m * 4 + 4, :] = rows[i * 32 + z * 4 : i * 32 + z * 4 + 4, :]
 
     @pl.when(core == 1)
     def _():
-        for i in range(8):
-            for z in range(8):
-                source, dest = (i * 8 + z) * 4, (z * 8 + i) * 4
-                out_ref[dest : dest + 4, :] = rows[source : source + 4, :]
+        for k, z in enumerate(LINE_ORDER):
+            for m, i in enumerate(PLANE_ORDER):
+                out_ref[k * 32 + m * 4 : k * 32 + m * 4 + 4, :] = rows[i * 32 + z * 4 : i * 32 + z * 4 + 4, :]
 
 
 def project(temps, area_weight, eofs):
@@ -114,9 +119,9 @@
     )(on_chip(parts))
 
 
-def place(block, dest_ref):
+def place(block, dest_ref, order):
     for source in range(16):
-        chan, half = source // 2, source % 2
+        half, chan = HALF_ORDER[source // 8], order[source % 8]
         for core in range(2):
             for seg in range(4):
                 row = core * 16 + seg * 4
@@ -134,8 +139,8 @@
     first_lag = (lax.axis_index("xh") * 2 + core) * LAGS_DEV
     mine = mine_ref[...]
     other = other_ref[...]
-    place(jnp.where(core == 0, mine, other), a_ref)
-    place(jnp.where(core == 0, other, mine), b_ref)
+    place(jnp.where(core == 0, mine, other), a_ref, PLANE_ORDER)
+    place(jnp.where(core == 0, other, mine), b_ref, LINE_ORDER)
     a = a_ref[...]
     a = a - jnp.sum(a, axis=1, keepdims=True) * (1.0 / HOURS)
     b = b_ref[:, :HOURS]
@@ -157,8 +162,8 @@
     for p in range(2):
         high, low = product[2 * p * TILE : (2 * p + 1) * TILE, :], product[(2 * p + 1) * TILE : (2 * p + 2) * TILE, :]
         tile = (high[:, :128] + low[:, :128] + high[:, 128:]) * (1.0 / HOURS)
-        for owner in range(8):
-            out_ref[owner, p * 4 : p * 4 + 4, :] = tile[owner * 4 : owner * 4 + 4, :]
+        for k, owner in enumerate(OUT_ORDER):
+            out_ref[k, p * 4 : p * 4 + 4, :] = tile[owner * 4 : owner * 4 + 4, :]
 
 
 def tiles(mine, other):
@@ -179,8 +184,8 @@
 def spread_kernel(parts_ref, out_ref):
     for lag in range(LAGS_DEV):
         row, lane = 4 * (lag // 4), TILE * (lag % 4)
-        for source in range(8):
-            out_ref[lag, :, source * TILE : (source + 1) * TILE] = parts_ref[source, row : row + 4, lane : lane + TILE]
+        for k, source in enumerate(OUT_ORDER):
+            out_ref[lag, :, source * TILE : (source + 1) * TILE] = parts_ref[k, row : row + 4, lane : lane + TILE]
 
 
 def spread(parts):
@@ -197,13 +202,20 @@
     return ((i * 8 + z) * 2 + xh) * 2 + core
 
 
-PLANES = [[[device(i, z, xh, core) for i in range(8)] for z in range(8) for xh in range(2)] for core in range(2)]
-LINES = [[[device(i, z, xh, core) for z in range(8)] for i in range(8) for xh in range(2)] for core in range(2)]
-FIRST_GROUPS = PLANES[0] + LINES[1]
-SECOND_GROUPS = LINES[0] + PLANES[1]
-GATHER_GROUPS = [[device(i, z, xh, 0) for i in range(8) for xh in range(2)] for z in range(8)] + [
-    [device(i, z, xh, 1) for z in range(8) for xh in range(2)] for i in range(8)
+def planes(core, order):
+    return [[device(i, z, xh, core) for i in order] for z in range(8) for xh in range(2)]
+
+
+def lines(core):
+    return [[device(i, z, xh, core) for z in LINE_ORDER] for i in range(8) for xh in range(2)]
+
+
+FIRST_GROUPS = planes(0, PLANE_ORDER) + lines(1)
+SECOND_GROUPS = lines(0) + planes(1, PLANE_ORDER)
+GATHER_GROUPS = [[device(i, z, xh, 0) for xh in HALF_ORDER for i in PLANE_ORDER] for z in range(8)] + [
+    [device(i, z, xh, 1) for xh in HALF_ORDER for z in LINE_ORDER] for i in range(8)
 ]
+OUT_GROUPS = planes(0, OUT_ORDER) + planes(1, OUT_ORDER)
 SWAP = [(0, 1), (1, 0)]
 
 
@@ -225,7 +237,7 @@
         jnp.broadcast_to(pair[None], (16, 32, 128)), AXES, 0, 0, axis_index_groups=GATHER_GROUPS
     )
     other = lax.ppermute(mine, "core", SWAP)
-    out = lax.all_to_all(tiles(mine, other), ("xl", "y"), 0, 0)
+    out = lax.all_to_all(tiles(mine, other), AXES, 0, 0, axis_index_groups=OUT_GROUPS)
     return spread(out)
 
 

time: 64 us -> 57.5 us (0.90)
  blocking collectives: 53.6 us -> 46.8 us
    all_to_all x1, blocking collectives: 21 us -> 17.2 us  [shards(): lax.all_to_all(partial_sums.reshape(8, TILE, HOURS_DEV), AXES, 0, 0, axis...]
    all_to_all x1, blocking collectives: 10.4 us -> 8.29 us  [shards(): lax.all_to_all(sum_rows(parts), AXES, 0, 0, axis_index_groups=SECOND_GROUPS)]
where the time goes in v5:
time: 57.5 us; the launch traced here: 57.2 us
  blocking collectives  46.8 us (81%)
  Pallas kernels  7.1 us (12%)
  waiting for transfers between devices  2.36 us (4%)
  starting transfers between devices  0.84 us (1%)
    all_to_all x1, blocking collectives, shards(): lax.all_to_all(partial_sums.reshape(8, TILE, HOURS_DEV), AXES, 0, 0, axis...  17.2 us
    all_to_all x1, blocking collectives, shards(): lax.all_to_all(jnp.broadcast_to(pair[None], (16, 32, 128)), AXES, 0, 0, a...  14.3 us
    all_to_all x1, blocking collectives, shards(): lax.all_to_all(sum_rows(parts), AXES, 0, 0, axis_index_groups=SECOND_GROUPS)  8.29 us
    all_to_all x1, blocking collectives, shards(): lax.all_to_all(tiles(mine, other), AXES, 0, 0, axis_index_groups=OUT_GROUPS)  7.1 us
    pallas_call x1, Pallas kernels, project(): pl.pallas_call(project_kernel, in_specs=[ANY_SPEC, ANY_SPEC, ANY_SPEC], o...  5.44 us
    ppermute x1, waiting for transfers between devices, shards(): other = lax.ppermute(mine, 'core', SWAP)  1.53 us
  transfers between devices with their start and end apart: 2, of which 2 were waited for; matrix products, arithmetic and copies ran while one was open for 0% of the time, Pallas kernels for 0%

profile of v5, /device:TPU:1, one launch (start us, length us, event | category | flops | bytes accessed | tf_op | source)
XLA Modules:
  0.0 57.2 jit_solution(12724871112570379026)
XLA Ops:
  0.0 5.4 %project.1 = f32[256,512]{1,0:T(8,128)S(1)} custom-call(f32[512,4096]{1,0:T(8,128)} %temps_hbm.1, f32[32,128]{1,0:T(8,128)} %bitcast.3, bf16[4096,256]{1,0:T(8,128)(2,1)} %eofs_hbm.1), custom_call_target="tpu_custom_call" | custom-call | tf_op jit(solution)/shard_map/project/pallas_call | solution.py:87
  5.5 17.2 %all_to_all.20.parts_ref = f32[8,32,512]{2,1,0:T(8,128)S(1)} all-to-all(f32[8,32,512]{2,1,0:T(8,128)S(1)} %bitcast.2), channel_id=1, replica_groups={{192,160,128,224,64,32,0,96},{194,162,130,226,66,34,2,98},{196,164,132,..., dimensions={0} | all-to-all | bytes 1048576 | tf_op jit(solution)/shard_map/all_to_all | solution.py:224
  22.6 8.3 %all_to_all.21 = f32[8,16,128]{2,1,0:T(8,128)S(1)} all-to-all(f32[8,16,128]{2,1,0:T(8,128)S(1)} %sum_rows.1), channel_id=1, replica_groups={{16,12,8,4,0,28,24,20},{18,14,10,6,2,30,26,22},{48,44,40,36,32,60,56,52..., dimensions={0} | all-to-all | bytes 131072 | tf_op jit(solution)/shard_map/all_to_all | solution.py:227
  31.0 0.8 %collective-permute-start = (f32[16,128]{1,0:T(8,128)S(1)}, f32[16,128]{1,0:T(8,128)S(1)}, u32[]{:S(2)}, u32[]{:S(2)}) collective-permute-start(f32[16,128]{1,0:T(8,128)S(1)} %reduce_sum.9), channel_id=1, source_target_pairs={{0,1},{1,0},{2,3},{3,2},{4,5},{5,4},{6,7},{7,6},{8,9},{9,8},{10,11... | collective-permute-start | bytes 24584 | tf_op jit(solution)/shard_map/ppermute | solution.py:230
  31.8 0.8 %collective-permute-done = f32[16,128]{1,0:T(8,128)S(1)} collective-permute-done((f32[16,128]{1,0:T(8,128)S(1)}, f32[16,128]{1,0:T(8,128)S(1)}, u32[]{:S(2)}, u32[]{:S(2)}) %collective-permute-start) | collective-permute-done | bytes 8224 | tf_op jit(solution)/shard_map/ppermute | solution.py:230
  32.7 14.3 %all_to_all.22.mine_ref = f32[16,32,128]{2,1,0:T(8,128)S(1)} all-to-all(f32[16,32,128]{2,1,0:T(8,128)S(1)} %broadcast_in_dim.2), channel_id=1, replica_groups={{194,162,130,226,66,34,2,98,192,160,128,224,64,32,0,96},{198,166,134,23..., dimensions={0} | all-to-all | bytes 524288 | tf_op jit(solution)/shard_map/all_to_all | solution.py:236
  46.9 0.0 collective-permute-start.1
  46.9 1.5 %collective-permute-done.1.other_ref = f32[16,32,128]{2,1,0:T(8,128)S(1)} collective-permute-done((f32[16,32,128]{2,1,0:T(8,128)S(1)}, f32[16,32,128]{2,1,0:T(8,128)S(1)}, u32[]{:S(2)}, u32[]{:S(2)}) %collective-permute-start.1) | collective-permute-done | bytes 262176 | tf_op jit(solution)/shard_map/ppermute | solution.py:239
  48.5 0.9 %tiles.1 = f32[8,8,128]{2,1,0:T(8,128)S(1)} custom-call(f32[16,32,128]{2,1,0:T(8,128)S(1)} %all_to_all.22.mine_ref, f32[16,32,128]{2,1,0:T(8,128)S(1)} %collective-permute-done.1.other_ref), custom_call_target="tpu_custom_call" | custom-call | tf_op jit(solution)/shard_map/tiles/pallas_call | solution.py:170
  49.4 7.1 %all_to_all.23.parts_ref = f32[8,8,128]{2,1,0:T(8,128)S(1)} all-to-all(f32[8,8,128]{2,1,0:T(8,128)S(1)} %tiles.1), channel_id=1, replica_groups={{192,160,128,224,64,32,0,96},{194,162,130,226,66,34,2,98},{196,164,132,..., dimensions={0} | all-to-all | bytes 65536 | tf_op jit(solution)/shard_map/all_to_all | solution.py:240
  56.5 0.7 %spread.1 = f32[8,4,256]{2,1,0:T(4,128)} custom-call(f32[8,8,128]{2,1,0:T(8,128)S(1)} %all_to_all.23.parts_ref), custom_call_target="tpu_custom_call" | custom-call | tf_op jit(solution)/shard_map/spread/pallas_call | solution.py:192
  (4 shorter events, 0.1 us)
Async XLA Ops:
  31.0 1.7 %collective-permute-start = (f32[16,128]{1,0:T(8,128)S(1)}, f32[16,128]{1,0:T(8,128)S(1)}, u32[]{:S(2)}, u32[]{:S(2)}) collective-permute-start(f32[16,128]{1,0:T(8,128)S(1)} %reduce_sum.9), channel_id=1, source_target_pairs={{0,1},{1,0},{2,3},{3,2},{4,5},{5,4},{6,7},{7,6},{8,9},{9,8},{10,11... | collective-permute-start | bytes 24584 | tf_op jit(solution)/shard_map/ppermute | solution.py:230
  46.9 1.5 %collective-permute-start.1 = (f32[16,32,128]{2,1,0:T(8,128)S(1)}, f32[16,32,128]{2,1,0:T(8,128)S(1)}, u32[]{:S(2)}, u32[]{:S(2)}) collective-permute-start(f32[16,32,128]{2,1,0:T(8,128)S(1)} %all_to_all.22.mine_ref), channel_id=1, source_target_pairs={{0,1},{1,0},{2,3},{3,2},{4,5},{5,4},{6,7},{7,6},{8,9},{9,8},{10,11... | collective-permute-start | bytes 786440 | tf_op jit(solution)/shard_map/ppermute | solution.py:239

commit v6 on v5

--- a/solution.py
+++ b/solution.py
@@ -40,14 +40,14 @@
         for k in range(blocks)
     ]
     for k in range(COPIES_AHEAD):
-        temps_copies[k].start()
+        temps_copies[k].start(priority=k % 2)
         eofs_copies[k].start()
     weight_copy.wait()
     for k in range(blocks):
         temps_copies[k].wait()
         eofs_copies[k].wait()
         if k + COPIES_AHEAD < blocks:
-            temps_copies[k + COPIES_AHEAD].start()
+            temps_copies[k + COPIES_AHEAD].start(priority=k % 2)
             eofs_copies[k + COPIES_AHEAD].start()
         first = k * (COL_BLOCK // 128)
         column_weight = jnp.concatenate(

time: 57.5 us -> 57.2 us (level)
  no operation moved by 1% of the time
where the time goes in v6:
time: 57.2 us; the launch traced here: 57 us
  blocking collectives  46.8 us (82%)
  Pallas kernels  6.84 us (12%)
  waiting for transfers between devices  2.36 us (4%)
  starting transfers between devices  0.84 us (1%)
    all_to_all x1, blocking collectives, shards(): lax.all_to_all(partial_sums.reshape(8, TILE, HOURS_DEV), AXES, 0, 0, axis...  17.2 us
    all_to_all x1, blocking collectives, shards(): lax.all_to_all(jnp.broadcast_to(pair[None], (16, 32, 128)), AXES, 0, 0, a...  14.3 us
    all_to_all x1, blocking collectives, shards(): lax.all_to_all(sum_rows(parts), AXES, 0, 0, axis_index_groups=SECOND_GROUPS)  8.29 us
    all_to_all x1, blocking collectives, shards(): lax.all_to_all(tiles(mine, other), AXES, 0, 0, axis_index_groups=OUT_GROUPS)  7.1 us
    pallas_call x1, Pallas kernels, project(): pl.pallas_call(project_kernel, in_specs=[ANY_SPEC, ANY_SPEC, ANY_SPEC], o...  5.18 us
    ppermute x1, waiting for transfers between devices, shards(): other = lax.ppermute(mine, 'core', SWAP)  1.53 us
  transfers between devices with their start and end apart: 2, of which 2 were waited for; matrix products, arithmetic and copies ran while one was open for 0% of the time, Pallas kernels for 0%

profile of v6, /device:TPU:1, one launch (start us, length us, event | category | flops | bytes accessed | tf_op | source)
XLA Modules:
  0.0 57.0 jit_solution(5054571519840894142)
XLA Ops:
  0.0 5.2 %project.1 = f32[256,512]{1,0:T(8,128)S(1)} custom-call(f32[512,4096]{1,0:T(8,128)} %temps_hbm.1, f32[32,128]{1,0:T(8,128)} %bitcast.3, bf16[4096,256]{1,0:T(8,128)(2,1)} %eofs_hbm.1), custom_call_target="tpu_custom_call" | custom-call | tf_op jit(solution)/shard_map/project/pallas_call | solution.py:87
  5.2 17.2 %all_to_all.20.parts_ref = f32[8,32,512]{2,1,0:T(8,128)S(1)} all-to-all(f32[8,32,512]{2,1,0:T(8,128)S(1)} %bitcast.2), channel_id=1, replica_groups={{192,160,128,224,64,32,0,96},{194,162,130,226,66,34,2,98},{196,164,132,..., dimensions={0} | all-to-all | bytes 1048576 | tf_op jit(solution)/shard_map/all_to_all | solution.py:224
  22.4 8.3 %all_to_all.21 = f32[8,16,128]{2,1,0:T(8,128)S(1)} all-to-all(f32[8,16,128]{2,1,0:T(8,128)S(1)} %sum_rows.1), channel_id=1, replica_groups={{16,12,8,4,0,28,24,20},{18,14,10,6,2,30,26,22},{48,44,40,36,32,60,56,52..., dimensions={0} | all-to-all | bytes 131072 | tf_op jit(solution)/shard_map/all_to_all | solution.py:227
  30.7 0.8 %collective-permute-start = (f32[16,128]{1,0:T(8,128)S(1)}, f32[16,128]{1,0:T(8,128)S(1)}, u32[]{:S(2)}, u32[]{:S(2)}) collective-permute-start(f32[16,128]{1,0:T(8,128)S(1)} %reduce_sum.9), channel_id=1, source_target_pairs={{0,1},{1,0},{2,3},{3,2},{4,5},{5,4},{6,7},{7,6},{8,9},{9,8},{10,11... | collective-permute-start | bytes 24584 | tf_op jit(solution)/shard_map/ppermute | solution.py:230
  31.5 0.8 %collective-permute-done = f32[16,128]{1,0:T(8,128)S(1)} collective-permute-done((f32[16,128]{1,0:T(8,128)S(1)}, f32[16,128]{1,0:T(8,128)S(1)}, u32[]{:S(2)}, u32[]{:S(2)}) %collective-permute-start) | collective-permute-done | bytes 8224 | tf_op jit(solution)/shard_map/ppermute | solution.py:230
  32.4 14.3 %all_to_all.22.mine_ref = f32[16,32,128]{2,1,0:T(8,128)S(1)} all-to-all(f32[16,32,128]{2,1,0:T(8,128)S(1)} %broadcast_in_dim.2), channel_id=1, replica_groups={{194,162,130,226,66,34,2,98,192,160,128,224,64,32,0,96},{198,166,134,23..., dimensions={0} | all-to-all | bytes 524288 | tf_op jit(solution)/shard_map/all_to_all | solution.py:236
  46.7 0.0 collective-permute-start.1
  46.7 1.5 %collective-permute-done.1.other_ref = f32[16,32,128]{2,1,0:T(8,128)S(1)} collective-permute-done((f32[16,32,128]{2,1,0:T(8,128)S(1)}, f32[16,32,128]{2,1,0:T(8,128)S(1)}, u32[]{:S(2)}, u32[]{:S(2)}) %collective-permute-start.1) | collective-permute-done | bytes 262176 | tf_op jit(solution)/shard_map/ppermute | solution.py:239
  48.2 0.9 %tiles.1 = f32[8,8,128]{2,1,0:T(8,128)S(1)} custom-call(f32[16,32,128]{2,1,0:T(8,128)S(1)} %all_to_all.22.mine_ref, f32[16,32,128]{2,1,0:T(8,128)S(1)} %collective-permute-done.1.other_ref), custom_call_target="tpu_custom_call" | custom-call | tf_op jit(solution)/shard_map/tiles/pallas_call | solution.py:170
  49.1 7.1 %all_to_all.23.parts_ref = f32[8,8,128]{2,1,0:T(8,128)S(1)} all-to-all(f32[8,8,128]{2,1,0:T(8,128)S(1)} %tiles.1), channel_id=1, replica_groups={{192,160,128,224,64,32,0,96},{194,162,130,226,66,34,2,98},{196,164,132,..., dimensions={0} | all-to-all | bytes 65536 | tf_op jit(solution)/shard_map/all_to_all | solution.py:240
  56.2 0.7 %spread.1 = f32[8,4,256]{2,1,0:T(4,128)} custom-call(f32[8,8,128]{2,1,0:T(8,128)S(1)} %all_to_all.23.parts_ref), custom_call_target="tpu_custom_call" | custom-call | tf_op jit(solution)/shard_map/spread/pallas_call | solution.py:192
  (4 shorter events, 0.1 us)
Async XLA Ops:
  30.7 1.7 %collective-permute-start = (f32[16,128]{1,0:T(8,128)S(1)}, f32[16,128]{1,0:T(8,128)S(1)}, u32[]{:S(2)}, u32[]{:S(2)}) collective-permute-start(f32[16,128]{1,0:T(8,128)S(1)} %reduce_sum.9), channel_id=1, source_target_pairs={{0,1},{1,0},{2,3},{3,2},{4,5},{5,4},{6,7},{7,6},{8,9},{9,8},{10,11... | collective-permute-start | bytes 24584 | tf_op jit(solution)/shard_map/ppermute | solution.py:230
  46.7 1.5 %collective-permute-start.1 = (f32[16,32,128]{2,1,0:T(8,128)S(1)}, f32[16,32,128]{2,1,0:T(8,128)S(1)}, u32[]{:S(2)}, u32[]{:S(2)}) collective-permute-start(f32[16,32,128]{2,1,0:T(8,128)S(1)} %all_to_all.22.mine_ref), channel_id=1, source_target_pairs={{0,1},{1,0},{2,3},{3,2},{4,5},{5,4},{6,7},{7,6},{8,9},{9,8},{10,11... | collective-permute-start | bytes 786440 | tf_op jit(solution)/shard_map/ppermute | solution.py:239

commit v7 on v6

--- a/solution.py
+++ b/solution.py
@@ -15,9 +15,9 @@
 CHANNELS = 256
 LAGS_DEV = 8
 TILE = 32
-LINE_ORDER = (4, 3, 2, 1, 0, 7, 6, 5)
-PLANE_ORDER = (6, 5, 4, 7, 2, 1, 0, 3)
-OUT_ORDER = (6, 5, 4, 7, 2, 1, 0, 3)
+LINE_ORDER = (4, 0, 3, 7, 2, 6, 1, 5)
+PLANE_ORDER = (6, 0, 5, 3, 4, 2, 7, 1)
+OUT_ORDER = (6, 0, 5, 3, 4, 2, 7, 1)
 HALF_ORDER = (1, 0)
 VMEM_SPEC = pl.BlockSpec(memory_space=pltpu.VMEM)
 ANY_SPEC = pl.BlockSpec(memory_space=pl.ANY)

time: 57.2 us -> 56.5 us (0.988)
    all_to_all x1, blocking collectives: 14.3 us -> 13.3 us  [shards(): lax.all_to_all(jnp.broadcast_to(pair[None], (16, 32, 128)), AXES, 0, 0, a...]
where the time goes in v7:
time: 56.5 us; the launch traced here: 56.3 us
  blocking collectives  46.5 us (82%)
  Pallas kernels  6.84 us (12%)
  waiting for transfers between devices  2.27 us (4%)
  starting transfers between devices  0.6 us (1%)
    all_to_all x1, blocking collectives, shards(): lax.all_to_all(partial_sums.reshape(8, TILE, HOURS_DEV), AXES, 0, 0, axis...  17.5 us
    all_to_all x1, blocking collectives, shards(): lax.all_to_all(jnp.broadcast_to(pair[None], (16, 32, 128)), AXES, 0, 0, a...  13.3 us
    all_to_all x1, blocking collectives, shards(): lax.all_to_all(sum_rows(parts), AXES, 0, 0, axis_index_groups=SECOND_GROUPS)  8.21 us
    all_to_all x1, blocking collectives, shards(): lax.all_to_all(tiles(mine, other), AXES, 0, 0, axis_index_groups=OUT_GROUPS)  7.41 us
    pallas_call x1, Pallas kernels, project(): pl.pallas_call(project_kernel, in_specs=[ANY_SPEC, ANY_SPEC, ANY_SPEC], o...  5.19 us
    ppermute x1, waiting for transfers between devices, shards(): other = lax.ppermute(mine, 'core', SWAP)  1.44 us
  transfers between devices with their start and end apart: 2, of which 2 were waited for; matrix products, arithmetic and copies ran while one was open for 0% of the time, Pallas kernels for 0%

profile of v7, /device:TPU:1, one launch (start us, length us, event | category | flops | bytes accessed | tf_op | source)
XLA Modules:
  0.0 56.3 jit_solution(1321411299571287420)
XLA Ops:
  0.0 5.2 %project.1 = f32[256,512]{1,0:T(8,128)S(1)} custom-call(f32[512,4096]{1,0:T(8,128)} %temps_hbm.1, f32[32,128]{1,0:T(8,128)} %bitcast.3, bf16[4096,256]{1,0:T(8,128)(2,1)} %eofs_hbm.1), custom_call_target="tpu_custom_call" | custom-call | tf_op jit(solution)/shard_map/project/pallas_call | solution.py:87
  5.2 17.5 %all_to_all.20.parts_ref = f32[8,32,512]{2,1,0:T(8,128)S(1)} all-to-all(f32[8,32,512]{2,1,0:T(8,128)S(1)} %bitcast.2), channel_id=1, replica_groups={{192,0,160,96,128,64,224,32},{194,2,162,98,130,66,226,34},{196,4,164,10..., dimensions={0} | all-to-all | bytes 1048576 | tf_op jit(solution)/shard_map/all_to_all | solution.py:224
  22.7 8.2 %all_to_all.21 = f32[8,16,128]{2,1,0:T(8,128)S(1)} all-to-all(f32[8,16,128]{2,1,0:T(8,128)S(1)} %sum_rows.1), channel_id=1, replica_groups={{16,0,12,28,8,24,4,20},{18,2,14,30,10,26,6,22},{48,32,44,60,40,56,36,52..., dimensions={0} | all-to-all | bytes 131072 | tf_op jit(solution)/shard_map/all_to_all | solution.py:227
  31.0 0.5 collective-permute-start
  31.5 0.8 %collective-permute-done = f32[16,128]{1,0:T(8,128)S(1)} collective-permute-done((f32[16,128]{1,0:T(8,128)S(1)}, f32[16,128]{1,0:T(8,128)S(1)}, u32[]{:S(2)}, u32[]{:S(2)}) %collective-permute-start) | collective-permute-done | bytes 8224 | tf_op jit(solution)/shard_map/ppermute | solution.py:230
  32.3 13.3 %all_to_all.22.mine_ref = f32[16,32,128]{2,1,0:T(8,128)S(1)} all-to-all(f32[16,32,128]{2,1,0:T(8,128)S(1)} %broadcast_in_dim.2), channel_id=1, replica_groups={{194,2,162,98,130,66,226,34,192,0,160,96,128,64,224,32},{198,6,166,102,..., dimensions={0} | all-to-all | bytes 524288 | tf_op jit(solution)/shard_map/all_to_all | solution.py:236
  45.7 0.1 collective-permute-start.1
  45.8 1.4 %collective-permute-done.1.other_ref = f32[16,32,128]{2,1,0:T(8,128)S(1)} collective-permute-done((f32[16,32,128]{2,1,0:T(8,128)S(1)}, f32[16,32,128]{2,1,0:T(8,128)S(1)}, u32[]{:S(2)}, u32[]{:S(2)}) %collective-permute-start.1) | collective-permute-done | bytes 262176 | tf_op jit(solution)/shard_map/ppermute | solution.py:239
  47.2 0.9 %tiles.1 = f32[8,8,128]{2,1,0:T(8,128)S(1)} custom-call(f32[16,32,128]{2,1,0:T(8,128)S(1)} %all_to_all.22.mine_ref, f32[16,32,128]{2,1,0:T(8,128)S(1)} %collective-permute-done.1.other_ref), custom_call_target="tpu_custom_call" | custom-call | tf_op jit(solution)/shard_map/tiles/pallas_call | solution.py:170
  48.1 7.4 %all_to_all.23.parts_ref = f32[8,8,128]{2,1,0:T(8,128)S(1)} all-to-all(f32[8,8,128]{2,1,0:T(8,128)S(1)} %tiles.1), channel_id=1, replica_groups={{192,0,160,96,128,64,224,32},{194,2,162,98,130,66,226,34},{196,4,164,10..., dimensions={0} | all-to-all | bytes 65536 | tf_op jit(solution)/shard_map/all_to_all | solution.py:240
  55.5 0.7 %spread.1 = f32[8,4,256]{2,1,0:T(4,128)} custom-call(f32[8,8,128]{2,1,0:T(8,128)S(1)} %all_to_all.23.parts_ref), custom_call_target="tpu_custom_call" | custom-call | tf_op jit(solution)/shard_map/spread/pallas_call | solution.py:192
  (4 shorter events, 0.1 us)
Async XLA Ops:
  31.0 1.3 %collective-permute-start = (f32[16,128]{1,0:T(8,128)S(1)}, f32[16,128]{1,0:T(8,128)S(1)}, u32[]{:S(2)}, u32[]{:S(2)}) collective-permute-start(f32[16,128]{1,0:T(8,128)S(1)} %reduce_sum.9), channel_id=1, source_target_pairs={{0,1},{1,0},{2,3},{3,2},{4,5},{5,4},{6,7},{7,6},{8,9},{9,8},{10,11... | collective-permute-start | bytes 24584 | tf_op jit(solution)/shard_map/ppermute | solution.py:230
  45.7 1.5 %collective-permute-start.1 = (f32[16,32,128]{2,1,0:T(8,128)S(1)}, f32[16,32,128]{2,1,0:T(8,128)S(1)}, u32[]{:S(2)}, u32[]{:S(2)}) collective-permute-start(f32[16,32,128]{2,1,0:T(8,128)S(1)} %all_to_all.22.mine_ref), channel_id=1, source_target_pairs={{0,1},{1,0},{2,3},{3,2},{4,5},{5,4},{6,7},{7,6},{8,9},{9,8},{10,11... | collective-permute-start | bytes 786440 | tf_op jit(solution)/shard_map/ppermute | solution.py:239

commit v8 on v7

--- a/solution.py
+++ b/solution.py
@@ -36,20 +36,24 @@
         for k in range(blocks)
     ]
     eofs_copies = [
-        pltpu.make_async_copy(eofs_hbm.at[pl.ds(k * COL_BLOCK, COL_BLOCK), :], eofs.at[k], eofs_sem.at[k])
-        for k in range(blocks)
+        pltpu.make_async_copy(eofs_hbm.at[pl.ds(k * 2 * COL_BLOCK, 2 * COL_BLOCK), :], eofs.at[k], eofs_sem.at[k])
+        for k in range(blocks // 2)
     ]
     for k in range(COPIES_AHEAD):
         temps_copies[k].start(priority=k % 2)
-        eofs_copies[k].start()
+        if k % 2 == 0:
+            eofs_copies[k // 2].start()
     weight_copy.wait()
     for k in range(blocks):
         temps_copies[k].wait()
-        eofs_copies[k].wait()
+        if k % 2 == 0:
+            eofs_copies[k // 2].wait()
         if k + COPIES_AHEAD < blocks:
             temps_copies[k + COPIES_AHEAD].start(priority=k % 2)
-            eofs_copies[k + COPIES_AHEAD].start()
+            if k % 2 == 0:
+                eofs_copies[(k + COPIES_AHEAD) // 2].start()
         first = k * (COL_BLOCK // 128)
+        block_eofs = eofs[k // 2, (k % 2) * COL_BLOCK : (k % 2 + 1) * COL_BLOCK, :]
         column_weight = jnp.concatenate(
             [weight[first + j : first + j + 1, :] for j in range(COL_BLOCK // 128)], axis=1
         )
@@ -58,8 +62,8 @@
             weighted = temps[k, rows, :] * column_weight
             high = weighted.astype(jnp.bfloat16)
             low = (weighted - high.astype(jnp.float32)).astype(jnp.bfloat16)
-            product = jnp.dot(high, eofs[k], preferred_element_type=jnp.float32) + jnp.dot(
-                low, eofs[k], preferred_element_type=jnp.float32
+            product = jnp.dot(high, block_eofs, preferred_element_type=jnp.float32) + jnp.dot(
+                low, block_eofs, preferred_element_type=jnp.float32
             )
             if k:
                 acc_ref[rows, :] += product
@@ -92,10 +96,10 @@
         scratch_shapes=[
             pltpu.VMEM((blocks, HOURS_DEV, COL_BLOCK), jnp.float32),
             pltpu.VMEM((cols // 128, 128), jnp.float32),
-            pltpu.VMEM((blocks, COL_BLOCK, CHANNELS), jnp.bfloat16),
+            pltpu.VMEM((blocks // 2, 2 * COL_BLOCK, CHANNELS), jnp.bfloat16),
             pltpu.VMEM((HOURS_DEV, CHANNELS), jnp.float32),
             pltpu.SemaphoreType.DMA((blocks,)),
-            pltpu.SemaphoreType.DMA((blocks,)),
+            pltpu.SemaphoreType.DMA((blocks // 2,)),
             pltpu.SemaphoreType.DMA(()),
         ],
         name="project",

time: 56.5 us -> 56.5 us (level)
  no operation moved by 1% of the time
where the time goes in v8:
time: 56.5 us; the launch traced here: 56.2 us
  blocking collectives  46.5 us (82%)
  Pallas kernels  6.82 us (12%)
  waiting for transfers between devices  2.27 us (4%)
  starting transfers between devices  0.6 us (1%)
    all_to_all x1, blocking collectives, shards(): lax.all_to_all(partial_sums.reshape(8, TILE, HOURS_DEV), AXES, 0, 0, axis...  17.5 us
    all_to_all x1, blocking collectives, shards(): lax.all_to_all(jnp.broadcast_to(pair[None], (16, 32, 128)), AXES, 0, 0, a...  13.3 us
    all_to_all x1, blocking collectives, shards(): lax.all_to_all(sum_rows(parts), AXES, 0, 0, axis_index_groups=SECOND_GROUPS)  8.21 us
    all_to_all x1, blocking collectives, shards(): lax.all_to_all(tiles(mine, other), AXES, 0, 0, axis_index_groups=OUT_GROUPS)  7.41 us
    pallas_call x1, Pallas kernels, project(): pl.pallas_call(project_kernel, in_specs=[ANY_SPEC, ANY_SPEC, ANY_SPEC], o...  5.16 us
    ppermute x1, waiting for transfers between devices, shards(): other = lax.ppermute(mine, 'core', SWAP)  1.44 us
  transfers between devices with their start and end apart: 2, of which 2 were waited for; matrix products, arithmetic and copies ran while one was open for 0% of the time, Pallas kernels for 0%

profile of v8, /device:TPU:1, one launch (start us, length us, event | category | flops | bytes accessed | tf_op | source)
XLA Modules:
  0.0 56.2 jit_solution(9429624105207902791)
XLA Ops:
  0.0 5.2 %project.1 = f32[256,512]{1,0:T(8,128)S(1)} custom-call(f32[512,4096]{1,0:T(8,128)} %temps_hbm.1, f32[32,128]{1,0:T(8,128)} %bitcast.3, bf16[4096,256]{1,0:T(8,128)(2,1)} %eofs_hbm.1), custom_call_target="tpu_custom_call" | custom-call | tf_op jit(solution)/shard_map/project/pallas_call | solution.py:91
  5.2 17.5 %all_to_all.20.parts_ref = f32[8,32,512]{2,1,0:T(8,128)S(1)} all-to-all(f32[8,32,512]{2,1,0:T(8,128)S(1)} %bitcast.2), channel_id=1, replica_groups={{192,0,160,96,128,64,224,32},{194,2,162,98,130,66,226,34},{196,4,164,10..., dimensions={0} | all-to-all | bytes 1048576 | tf_op jit(solution)/shard_map/all_to_all | solution.py:228
  22.7 8.2 %all_to_all.21 = f32[8,16,128]{2,1,0:T(8,128)S(1)} all-to-all(f32[8,16,128]{2,1,0:T(8,128)S(1)} %sum_rows.1), channel_id=1, replica_groups={{16,0,12,28,8,24,4,20},{18,2,14,30,10,26,6,22},{48,32,44,60,40,56,36,52..., dimensions={0} | all-to-all | bytes 131072 | tf_op jit(solution)/shard_map/all_to_all | solution.py:231
  30.9 0.5 collective-permute-start
  31.5 0.8 %collective-permute-done = f32[16,128]{1,0:T(8,128)S(1)} collective-permute-done((f32[16,128]{1,0:T(8,128)S(1)}, f32[16,128]{1,0:T(8,128)S(1)}, u32[]{:S(2)}, u32[]{:S(2)}) %collective-permute-start) | collective-permute-done | bytes 8224 | tf_op jit(solution)/shard_map/ppermute | solution.py:234
  32.3 13.3 %all_to_all.22.mine_ref = f32[16,32,128]{2,1,0:T(8,128)S(1)} all-to-all(f32[16,32,128]{2,1,0:T(8,128)S(1)} %broadcast_in_dim.2), channel_id=1, replica_groups={{194,2,162,98,130,66,226,34,192,0,160,96,128,64,224,32},{198,6,166,102,..., dimensions={0} | all-to-all | bytes 524288 | tf_op jit(solution)/shard_map/all_to_all | solution.py:240
  45.6 0.1 collective-permute-start.1
  45.7 1.4 %collective-permute-done.1.other_ref = f32[16,32,128]{2,1,0:T(8,128)S(1)} collective-permute-done((f32[16,32,128]{2,1,0:T(8,128)S(1)}, f32[16,32,128]{2,1,0:T(8,128)S(1)}, u32[]{:S(2)}, u32[]{:S(2)}) %collective-permute-start.1) | collective-permute-done | bytes 262176 | tf_op jit(solution)/shard_map/ppermute | solution.py:243
  47.2 0.9 %tiles.1 = f32[8,8,128]{2,1,0:T(8,128)S(1)} custom-call(f32[16,32,128]{2,1,0:T(8,128)S(1)} %all_to_all.22.mine_ref, f32[16,32,128]{2,1,0:T(8,128)S(1)} %collective-permute-done.1.other_ref), custom_call_target="tpu_custom_call" | custom-call | tf_op jit(solution)/shard_map/tiles/pallas_call | solution.py:174
  48.1 7.4 %all_to_all.23.parts_ref = f32[8,8,128]{2,1,0:T(8,128)S(1)} all-to-all(f32[8,8,128]{2,1,0:T(8,128)S(1)} %tiles.1), channel_id=1, replica_groups={{192,0,160,96,128,64,224,32},{194,2,162,98,130,66,226,34},{196,4,164,10..., dimensions={0} | all-to-all | bytes 65536 | tf_op jit(solution)/shard_map/all_to_all | solution.py:244
  55.5 0.7 %spread.1 = f32[8,4,256]{2,1,0:T(4,128)} custom-call(f32[8,8,128]{2,1,0:T(8,128)S(1)} %all_to_all.23.parts_ref), custom_call_target="tpu_custom_call" | custom-call | tf_op jit(solution)/shard_map/spread/pallas_call | solution.py:196
  (4 shorter events, 0.1 us)
Async XLA Ops:
  30.9 1.3 %collective-permute-start = (f32[16,128]{1,0:T(8,128)S(1)}, f32[16,128]{1,0:T(8,128)S(1)}, u32[]{:S(2)}, u32[]{:S(2)}) collective-permute-start(f32[16,128]{1,0:T(8,128)S(1)} %reduce_sum.9), channel_id=1, source_target_pairs={{0,1},{1,0},{2,3},{3,2},{4,5},{5,4},{6,7},{7,6},{8,9},{9,8},{10,11... | collective-permute-start | bytes 24584 | tf_op jit(solution)/shard_map/ppermute | solution.py:234
  45.6 1.5 %collective-permute-start.1 = (f32[16,32,128]{2,1,0:T(8,128)S(1)}, f32[16,32,128]{2,1,0:T(8,128)S(1)}, u32[]{:S(2)}, u32[]{:S(2)}) collective-permute-start(f32[16,32,128]{2,1,0:T(8,128)S(1)} %all_to_all.22.mine_ref), channel_id=1, source_target_pairs={{0,1},{1,0},{2,3},{3,2},{4,5},{5,4},{6,7},{7,6},{8,9},{9,8},{10,11... | collective-permute-start | bytes 786440 | tf_op jit(solution)/shard_map/ppermute | solution.py:243
